TPU v7x, 32 devices: a whole 2x2x4 slice. The times are simulated.
32 devices in a mesh: dp: 4 (over y, core), ctx: 4 (over z), tp: 2 (over x).
Axes of the slice: x: 2, y: 2, z: 4, core: 2. Of those that a mesh axis runs over, the one named last changes fastest.
Arguments:
- query_rows: bfloat16 [2048, 128, 128], P(('dp', 'ctx'), 'tp'), parts along dimension 0, may hold values from -6 to 6
- key_rows: bfloat16 [2048, 8, 128], P(('dp', 'ctx'), 'tp'), parts along dimension 0, may hold values from -6 to 6
- value_rows: bfloat16 [2048, 8, 128], P(('dp', 'ctx'), 'tp'), parts along dimension 0, may hold values from -6 to 6
- out_grad: bfloat16 [2048, 128, 128], P(('dp', 'ctx'), 'tp'), parts along dimension 0, may hold values from -6 to 6
- softmax_delta: float32 [2, 64, 2048], P('tp', 'ctx', 'dp'), parts along dimension 2, may hold values from -4 to 4
- log_norm: float32 [2, 64, 2048], P('tp', 'ctx', 'dp'), parts along dimension 2
- doc_lengths: int32 [12], P('dp'), parts along dimension 0, may hold values from 1 to 384, as said below
Outputs:
- query_grad: bfloat16 [2048, 128, 128], P(('dp', 'ctx'), 'tp'), parts along dimension 0
- key_grad: bfloat16 [2048, 8, 128], P(('dp', 'ctx'), 'tp'), parts along dimension 0
- value_grad: bfloat16 [2048, 8, 128], P(('dp', 'ctx'), 'tp'), parts along dimension 0
There are 4 independent parts, one for each index of `dp`. A program takes and returns all parts, laid end to end along the dimension named above; each array names one. Nothing has to cross between parts.
Inputs may be any that keep to these rules, and one draw needn't show every extreme that they name: `doc_lengths`: the 3 lengths sum to 512.
All inputs are finite; a program needn't handle non-finite values.
Results may differ from a plain program's by a relative error of at most 0.0056.
Values may be sent and summed in bfloat16 or wider, within the bound.
No kernel may reach another device: no remote copies, remote signals or barrier semaphores. Data moves between devices by JAX's collectives and lax.ppermute only.
A program may use at most 64 MiB of HBM per device.

v0:
```python
import functools

import jax
import jax.numpy as jnp
from jax import lax
from jax.experimental import pallas as pl
from jax.experimental.pallas import tpu as pltpu
from jax.sharding import PartitionSpec as P

DOC_MAX = 384
LOG2E = 1.4426950408889634


def dot_nt(left, right):
    return lax.dot_general(left, right, (((1,), (1,)), ((), ())), preferred_element_type=jnp.float32)


def dot_nn(left, right):
    return lax.dot_general(left, right, (((1,), (0,)), ((), ())), preferred_element_type=jnp.float32)


def doc_starts(docs_ref, n_docs, row_tok):
    start = jnp.zeros_like(row_tok)
    end = jnp.int32(0)
    for d in range(n_docs):
        end = end + docs_ref[d]
        start = jnp.where(row_tok >= end, jnp.maximum(start, end), start)
    return start


def pair_kernel(shifts, n_docs, share, docs_ref, q_ref, g_ref, norm_ref, delta_ref, *refs):
    n = len(shifts)
    kv_refs, ds_refs, out_refs = refs[:n], refs[n : 2 * n], refs[2 * n :]
    tok, _, dim = q_ref.shape
    rows = tok * share
    keys = kv_refs[0].shape[2]
    scaling = dim ** (-0.5)
    chunk = lax.axis_index("ctx")
    q = q_ref[...].reshape(rows, dim)
    g = g_ref[...].reshape(rows, dim)
    row = lax.broadcasted_iota(jnp.int32, (1, rows), 1)
    row_tok = chunk * tok + row // share
    start = doc_starts(docs_ref, n_docs, row_tok)
    norm = norm_ref[0] * LOG2E
    delta = delta_ref[0]
    block = 512
    for s, kv_ref, ds_ref, out_ref in zip(shifts, kv_refs, ds_refs, out_refs):
        k = kv_ref[0, 0]
        v = kv_ref[1, 0]
        base = (chunk - s) * tok
        first = start - base
        last = row_tok - base
        dk = jnp.zeros((keys, dim), jnp.float32)
        dv = jnp.zeros((keys, dim), jnp.float32)
        for b in range(rows // block):
            cut = slice(b * block, (b + 1) * block)
            key_pos = lax.broadcasted_iota(jnp.int32, (keys, block), 0)
            ok = key_pos >= first[:, cut]
            if s == 0:
                ok = ok & (key_pos <= last[:, cut])
            scores = dot_nt(k, q[cut])
            probs = jnp.where(ok, jnp.exp2(scores * (scaling * LOG2E) - norm[:, cut]), 0.0)
            dv = dv + dot_nn(probs.astype(jnp.bfloat16), g[cut])
            prob_grad = dot_nt(v, g[cut])
            ds = (probs * (prob_grad - delta[:, cut])).astype(jnp.bfloat16)
            ds_ref[0, :, cut] = ds
            dk = dk + dot_nn(ds, q[cut])
        out_ref[0, 0] = (dk * scaling).astype(out_ref.dtype)
        out_ref[1, 0] = dv.astype(out_ref.dtype)


def pair_grads(shifts, docs, q, g, norm, delta, kvs, out_types):
    tok, heads, dim = q.shape
    kv_heads = kvs[0].shape[1]
    share = heads // kv_heads
    rows = tok * share
    keys = kvs[0].shape[2]
    n = len(shifts)
    q_spec = pl.BlockSpec((tok, share, dim), lambda i, d: (0, i, 0))
    row_spec = pl.BlockSpec((1, 1, rows), lambda i, d: (i, 0, 0))
    kv_spec = pl.BlockSpec((2, 1, keys, dim), lambda i, d: (0, i, 0, 0))
    ds_spec = pl.BlockSpec((1, keys, rows), lambda i, d: (i, 0, 0))
    out = pl.pallas_call(
        functools.partial(pair_kernel, shifts, docs.shape[0], share),
        grid_spec=pltpu.PrefetchScalarGridSpec(
            num_scalar_prefetch=1,
            grid=(kv_heads,),
            in_specs=[q_spec, q_spec, row_spec, row_spec] + [kv_spec] * n,
            out_specs=[ds_spec] * n + [kv_spec] * n,
        ),
        out_shape=[jax.ShapeDtypeStruct((kv_heads, keys, rows), jnp.bfloat16)] * n
        + [jax.ShapeDtypeStruct((2, kv_heads, keys, dim), t) for t in out_types],
        cost_estimate=pl.CostEstimate(
            flops=8 * n * kv_heads * keys * rows * dim,
            transcendentals=n * kv_heads * keys * rows,
            bytes_accessed=4 * tok * heads * dim + 2 * n * kv_heads * keys * rows,
        ),
        name="pair_" + "_".join(str(s) for s in shifts),
    )(docs, q, g, norm, delta, *kvs)
    return out[:n], out[n:]


def query_kernel(share, *refs):
    n = (len(refs) - 1) // 2
    ds_refs, kv_refs, out_ref = refs[:n], refs[n : 2 * n], refs[-1]
    tok, _, dim = out_ref.shape
    scaling = dim ** (-0.5)
    ds = jnp.concatenate([r[0] for r in ds_refs], axis=0)
    k = jnp.concatenate([r[0, 0] for r in kv_refs], axis=0)
    total = lax.dot_general(ds, k, (((0,), (0,)), ((), ())), preferred_element_type=jnp.float32)
    out_ref[...] = (total * scaling).astype(jnp.bfloat16).reshape(tok, share, dim)


def query_grads(ds_list, kvs, tok):
    kv_heads, keys, rows = ds_list[0].shape
    dim = kvs[0].shape[3]
    share = rows // tok
    n = len(kvs)
    return pl.pallas_call(
        functools.partial(query_kernel, share),
        grid=(kv_heads,),
        in_specs=[pl.BlockSpec((1, keys, rows), lambda i: (i, 0, 0))] * n
        + [pl.BlockSpec((1, 1, keys, dim), lambda i: (0, i, 0, 0))] * n,
        out_specs=pl.BlockSpec((tok, share, dim), lambda i: (0, i, 0)),
        out_shape=jax.ShapeDtypeStruct((tok, kv_heads * share, dim), jnp.bfloat16),
        cost_estimate=pl.CostEstimate(
            flops=2 * n * kv_heads * keys * rows * dim,
            transcendentals=0,
            bytes_accessed=2 * n * kv_heads * keys * rows,
        ),
        name="query_grads",
    )(*ds_list, *kvs)


def local(query_rows, key_rows, value_rows, out_grad, softmax_delta, log_norm, doc_lengths):
    groups = lax.axis_size("ctx")
    tok, heads, dim = query_rows.shape
    kv_heads = key_rows.shape[1]
    share = heads // kv_heads
    per_dev = heads // groups
    reach = min(groups - 1, -(-(DOC_MAX - 1) // tok))
    own = jnp.stack([key_rows, value_rows]).transpose(0, 2, 1, 3)

    def moved(x, s):
        pairs = [(i, i + s) for i in range(groups) if 0 <= i + s < groups]
        return lax.ppermute(x, "ctx", pairs)

    kvs = [own] + [moved(own, s) for s in range(1, reach + 1)]
    stats = jnp.stack([log_norm[0], softmax_delta[0]])
    stats = stats.reshape(2, per_dev, groups, tok).transpose(2, 0, 3, 1)
    stats = lax.all_to_all(stats, "ctx", split_axis=0, concat_axis=0, tiled=True)
    stats = stats.reshape(kv_heads, groups // kv_heads, 2, tok, per_dev)
    stats = stats.transpose(2, 0, 3, 1, 4).reshape(2, kv_heads, 1, tok * share)
    norm, delta = stats[0], stats[1]

    def grads(shifts, types):
        return pair_grads(
            shifts, doc_lengths, query_rows, out_grad, norm, delta, [kvs[s] for s in shifts], types
        )

    ds_list, back = grads((0, 1), (jnp.float32, jnp.bfloat16))
    total = back[0]
    terms = [moved(back[1], -1)]
    for s in range(2, reach + 1):
        ds, part = grads((s,), (jnp.bfloat16,))
        ds_list = ds_list + ds
        terms.append(moved(part[0], -s))
    query_grad = query_grads(ds_list, kvs, tok)
    for term in terms:
        total = total + term.astype(jnp.float32)
    total = total.astype(jnp.bfloat16).transpose(0, 2, 1, 3)
    return (query_grad, total[0], total[1])


def solution(mesh):
    rows = P(("dp", "ctx"), "tp", None)
    stats = P("tp", "ctx", "dp")
    return jax.shard_map(
        local,
        mesh=mesh,
        in_specs=(rows, rows, rows, rows, stats, stats, P("dp")),
        out_specs=(rows, rows, rows),
        check_vma=False,
    )
```

profile of v0, /device:TPU:0, one launch (start us, length us, event | category | flops | bytes accessed | tf_op | source)
XLA Modules:
  0.0 79.9 jit_solution(5702765997578730427)
XLA Ops:
  0.6 0.8 pad_maximum_fusion
  1.4 0.6 copy.38
  2.1 6.3 %all-to-all-start = ((f32[4,2,128,16]{2,3,1,0:T(8,128)}), f32[4,2,128,16]{2,3,1,0:T(8,128)S(1)}, u32[]{:S(2)}, u32[]{:S(2)}) async-start(f32[4,2,128,16]{2,3,1,0:T(8,128)} %copy.38), calls=%async_computation | async-start | bytes 131072 | tf_op jit(solution)/shard_map/all_to_all | solution.py:151
  8.4 1.0 %copy_bitcast_fusion = (bf16[1,128,4,128]{3,1,2,0:T(8,128)(2,1)S(1)}, bf16[1,128,4,128]{3,1,2,0:T(8,128)(2,1)S(1)}) fusion(bf16[128,4,128]{2,1,0:T(4,128)(2,1)} %param.9, bf16[128,4,128]{2,1,0:T(4,128)(2,1)} %param.8), kind=kLoop, calls=%fused_computation.5 | loop fusion | bytes 524288 | tf_op jit(solution)/shard_map/stack | solution.py:142
  9.5 0.0 copy-start.2
  9.5 3.9 %collective-permute-start = (bf16[2,4,128,128]{3,2,1,0:T(8,128)(2,1)S(1)}, bf16[2,4,128,128]{3,2,1,0:T(8,128)(2,1)S(1)}, u32[]{:S(2)}, u32[]{:S(2)}) collective-permute-start(bf16[2,4,128,128]{3,2,1,0:T(8,128)(2,1)S(1)} %maximum_bitcast_fusion.refs_0_.refs_4_), channel_id=1, source_target_pairs={{0,2},{2,4},{4,6},{1,3},{3,5},{5,7},{8,10},{10,12},{12,14},{9,11},... | collective-permute-start | bytes 786440 | tf_op jit(solution)/shard_map/ppermute | solution.py:146
  13.4 4.3 %collective-permute-start.1 = (bf16[2,4,128,128]{3,2,1,0:T(8,128)(2,1)S(1)}, bf16[2,4,128,128]{3,2,1,0:T(8,128)(2,1)S(1)}, u32[]{:S(2)}, u32[]{:S(2)}) collective-permute-start(bf16[2,4,128,128]{3,2,1,0:T(8,128)(2,1)S(1)} %maximum_bitcast_fusion.refs_0_.refs_4_), channel_id=1, source_target_pairs={{0,4},{2,6},{1,5},{3,7},{8,12},{10,14},{9,13},{11,15},{16,20},{18,... | collective-permute-start | bytes 786440 | tf_op jit(solution)/shard_map/ppermute | solution.py:146
  17.7 1.3 %collective-permute-start.2 = (bf16[2,4,128,128]{3,2,1,0:T(8,128)(2,1)S(1)}, bf16[2,4,128,128]{3,2,1,0:T(8,128)(2,1)S(1)}, u32[]{:S(2)}, u32[]{:S(2)}) collective-permute-start(bf16[2,4,128,128]{3,2,1,0:T(8,128)(2,1)S(1)} %maximum_bitcast_fusion.refs_0_.refs_4_), channel_id=1, source_target_pairs={{0,6},{1,7},{8,14},{9,15},{16,22},{17,23},{24,30},{25,31}} | collective-permute-start | bytes 786440 | tf_op jit(solution)/shard_map/ppermute | solution.py:146
  19.0 0.0 all-to-all-done
  19.0 0.1 copy.39
  19.2 0.8 squeeze.16.norm_ref
  19.9 0.1 copy.40
  20.1 0.8 squeeze.17.delta_ref
  20.8 0.0 collective-permute-done.refs_1_.refs_5_
  20.8 0.0 copy-done.2
  20.8 0.0 copy-start.4
  20.8 0.7 copy-done.4
  21.6 13.6 %pair_0_1.1 = (bf16[4,128,2048]{2,1,0:T(8,128)(2,1)}, bf16[4,128,2048]{2,1,0:T(8,128)(2,1)}, f32[2,4,128,128]{3,2,1,0:T(8,128)}, bf16[2,4,128,128]{3,2,1,0:T(8,128)(2,1)}) custom-call(s32[3]{0:T(128)} %docs_ref.5, bf16[128,64,128]{2,1,0:T(8,128)(2,1)} %q_ref.5, bf16[128,64,128]{2,1,0:T(8,128)(2,1)} %g_ref.5, f32[4,1,2048]{2,1,0:T(1,128)} %squeeze.16.norm_ref, ...), custom_call_target="tpu_custom_call" | custom-call | flops 2147483648 | bytes 8388608 | tf_op jit(solution)/shard_map/pair_0_1/pallas_call | solution.py:83
  35.2 1.3 %collective-permute-start.3 = (bf16[2,4,128,128]{3,2,1,0:T(8,128)(2,1)}, bf16[2,4,128,128]{3,2,1,0:T(8,128)(2,1)S(1)}, u32[]{:S(2)}, u32[]{:S(2)}) collective-permute-start(bf16[2,4,128,128]{3,2,1,0:T(8,128)(2,1)} %get-tuple-element.16), channel_id=1, source_target_pairs={{2,0},{4,2},{6,4},{3,1},{5,3},{7,5},{10,8},{12,10},{14,12},{11,9},... | collective-permute-start | bytes 786440 | tf_op jit(solution)/shard_map/ppermute | solution.py:146
  36.5 0.0 collective-permute-done.1.refs_0_.refs_6_
  36.5 0.0 copy-start
  36.5 0.7 copy-done
  37.2 8.6 %pair_2.1 = (bf16[4,128,2048]{2,1,0:T(8,128)(2,1)}, bf16[2,4,128,128]{3,2,1,0:T(8,128)(2,1)}) custom-call(s32[3]{0:T(128)} %docs_ref.5, bf16[128,64,128]{2,1,0:T(8,128)(2,1)} %q_ref.5, bf16[128,64,128]{2,1,0:T(8,128)(2,1)} %g_ref.5, f32[4,1,2048]{2,1,0:T(1,128)} %squeeze.16.norm_ref, f32[4,1,2048]{2,1,0:T(1,128)} %squeeze.17.delta_ref, ...), custom_call_target="tpu_custom_call" | custom-call | flops 1073741824 | bytes 6291456 | tf_op jit(solution)/shard_map/pair_2/pallas_call | solution.py:83
  45.8 1.3 %collective-permute-start.4 = (bf16[2,4,128,128]{3,2,1,0:T(8,128)(2,1)}, bf16[2,4,128,128]{3,2,1,0:T(8,128)(2,1)S(1)}, u32[]{:S(2)}, u32[]{:S(2)}) collective-permute-start(bf16[2,4,128,128]{3,2,1,0:T(8,128)(2,1)} %get-tuple-element.17), channel_id=1, source_target_pairs={{4,0},{6,2},{5,1},{7,3},{12,8},{14,10},{13,9},{15,11},{20,16},{22,... | collective-permute-start | bytes 786440 | tf_op jit(solution)/shard_map/ppermute | solution.py:146
  47.1 0.0 collective-permute-done.2.refs_0_.refs_7_
  47.1 0.0 copy-start.1
  47.1 0.7 copy-done.1
  47.8 8.6 %pair_3.1 = (bf16[4,128,2048]{2,1,0:T(8,128)(2,1)}, bf16[2,4,128,128]{3,2,1,0:T(8,128)(2,1)}) custom-call(s32[3]{0:T(128)} %docs_ref.5, bf16[128,64,128]{2,1,0:T(8,128)(2,1)} %q_ref.5, bf16[128,64,128]{2,1,0:T(8,128)(2,1)} %g_ref.5, f32[4,1,2048]{2,1,0:T(1,128)} %squeeze.16.norm_ref, f32[4,1,2048]{2,1,0:T(1,128)} %squeeze.17.delta_ref, ...), custom_call_target="tpu_custom_call" | custom-call | flops 1073741824 | bytes 6291456 | tf_op jit(solution)/shard_map/pair_3/pallas_call | solution.py:83
  56.5 1.3 %collective-permute-start.5 = (bf16[2,4,128,128]{3,2,1,0:T(8,128)(2,1)}, bf16[2,4,128,128]{3,2,1,0:T(8,128)(2,1)S(1)}, u32[]{:S(2)}, u32[]{:S(2)}) collective-permute-start(bf16[2,4,128,128]{3,2,1,0:T(8,128)(2,1)} %get-tuple-element.18), channel_id=1, source_target_pairs={{6,0},{7,1},{14,8},{15,9},{22,16},{23,17},{30,24},{31,25}} | collective-permute-start | bytes 786440 | tf_op jit(solution)/shard_map/ppermute | solution.py:146
  57.8 0.0 copy-start.3
  57.8 6.8 %query_grads.1 = bf16[128,64,128]{2,1,0:T(8,128)(2,1)} custom-call(bf16[4,128,2048]{2,1,0:T(8,128)(2,1)} %get-tuple-element.11.refs_0_, bf16[4,128,2048]{2,1,0:T(8,128)(2,1)} %get-tuple-element.12.refs_1_, bf16[4,128,2048]{2,1,0:T(8,128)(2,1)} %get-tuple-element.13.refs_2_, bf16[4,128,2048]{2,1,0:T(8,128)(2,1)} %get-tuple-element.14.refs_3_, ...), custom_call_target="tpu_custom_call" | custom-call | flops 1073741824 | bytes 8388608 | tf_op jit(solution)/shard_map/query_grads/pallas_call | solution.py:119
  64.6 0.0 collective-permute-done.3
  64.6 6.4 %collective-permute-done.4 = bf16[2,4,128,128]{3,2,1,0:T(8,128)(2,1)S(1)} collective-permute-done((bf16[2,4,128,128]{3,2,1,0:T(8,128)(2,1)}, bf16[2,4,128,128]{3,2,1,0:T(8,128)(2,1)S(1)}, u32[]{:S(2)}, u32[]{:S(2)}) %collective-permute-start.4) | collective-permute-done | bytes 262176 | tf_op jit(solution)/shard_map/ppermute | solution.py:146
  71.0 7.2 %collective-permute-done.5 = bf16[2,4,128,128]{3,2,1,0:T(8,128)(2,1)S(1)} collective-permute-done((bf16[2,4,128,128]{3,2,1,0:T(8,128)(2,1)}, bf16[2,4,128,128]{3,2,1,0:T(8,128)(2,1)S(1)}, u32[]{:S(2)}, u32[]{:S(2)}) %collective-permute-start.5) | collective-permute-done | bytes 262176 | tf_op jit(solution)/shard_map/ppermute | solution.py:146
  78.2 0.0 copy-done.3
  78.2 0.1 fusion
  78.4 0.8 copy.49
  79.2 0.8 copy.50
  (4 shorter events, 0.1 us)
Async XLA Ops:
  2.1 16.9 %all-to-all-start = ((f32[4,2,128,16]{2,3,1,0:T(8,128)}), f32[4,2,128,16]{2,3,1,0:T(8,128)S(1)}, u32[]{:S(2)}, u32[]{:S(2)}) async-start(f32[4,2,128,16]{2,3,1,0:T(8,128)} %copy.38), calls=%async_computation | async-start | bytes 131072 | tf_op jit(solution)/shard_map/all_to_all | solution.py:151
  9.5 11.4 %copy-start.2 = (bf16[2,4,128,128]{3,2,1,0:T(8,128)(2,1)}, bf16[2,4,128,128]{3,2,1,0:T(8,128)(2,1)S(1)}, u32[]{:S(2)}) copy-start(bf16[2,4,128,128]{3,2,1,0:T(8,128)(2,1)S(1)} %maximum_bitcast_fusion.refs_0_.refs_4_) | copy-start | bytes 786436
  9.5 11.4 %collective-permute-start = (bf16[2,4,128,128]{3,2,1,0:T(8,128)(2,1)S(1)}, bf16[2,4,128,128]{3,2,1,0:T(8,128)(2,1)S(1)}, u32[]{:S(2)}, u32[]{:S(2)}) collective-permute-start(bf16[2,4,128,128]{3,2,1,0:T(8,128)(2,1)S(1)} %maximum_bitcast_fusion.refs_0_.refs_4_), channel_id=1, source_target_pairs={{0,2},{2,4},{4,6},{1,3},{3,5},{5,7},{8,10},{10,12},{12,14},{9,11},... | collective-permute-start | bytes 786440 | tf_op jit(solution)/shard_map/ppermute | solution.py:146
  13.4 23.1 %collective-permute-start.1 = (bf16[2,4,128,128]{3,2,1,0:T(8,128)(2,1)S(1)}, bf16[2,4,128,128]{3,2,1,0:T(8,128)(2,1)S(1)}, u32[]{:S(2)}, u32[]{:S(2)}) collective-permute-start(bf16[2,4,128,128]{3,2,1,0:T(8,128)(2,1)S(1)} %maximum_bitcast_fusion.refs_0_.refs_4_), channel_id=1, source_target_pairs={{0,4},{2,6},{1,5},{3,7},{8,12},{10,14},{9,13},{11,15},{16,20},{18,... | collective-permute-start | bytes 786440 | tf_op jit(solution)/shard_map/ppermute | solution.py:146
  17.7 29.4 %collective-permute-start.2 = (bf16[2,4,128,128]{3,2,1,0:T(8,128)(2,1)S(1)}, bf16[2,4,128,128]{3,2,1,0:T(8,128)(2,1)S(1)}, u32[]{:S(2)}, u32[]{:S(2)}) collective-permute-start(bf16[2,4,128,128]{3,2,1,0:T(8,128)(2,1)S(1)} %maximum_bitcast_fusion.refs_0_.refs_4_), channel_id=1, source_target_pairs={{0,6},{1,7},{8,14},{9,15},{16,22},{17,23},{24,30},{25,31}} | collective-permute-start | bytes 786440 | tf_op jit(solution)/shard_map/ppermute | solution.py:146
  20.8 0.7 copy-start.4
  35.2 29.4 %collective-permute-start.3 = (bf16[2,4,128,128]{3,2,1,0:T(8,128)(2,1)}, bf16[2,4,128,128]{3,2,1,0:T(8,128)(2,1)S(1)}, u32[]{:S(2)}, u32[]{:S(2)}) collective-permute-start(bf16[2,4,128,128]{3,2,1,0:T(8,128)(2,1)} %get-tuple-element.16), channel_id=1, source_target_pairs={{2,0},{4,2},{6,4},{3,1},{5,3},{7,5},{10,8},{12,10},{14,12},{11,9},... | collective-permute-start | bytes 786440 | tf_op jit(solution)/shard_map/ppermute | solution.py:146
  36.5 0.7 copy-start
  45.8 25.2 %collective-permute-start.4 = (bf16[2,4,128,128]{3,2,1,0:T(8,128)(2,1)}, bf16[2,4,128,128]{3,2,1,0:T(8,128)(2,1)S(1)}, u32[]{:S(2)}, u32[]{:S(2)}) collective-permute-start(bf16[2,4,128,128]{3,2,1,0:T(8,128)(2,1)} %get-tuple-element.17), channel_id=1, source_target_pairs={{4,0},{6,2},{5,1},{7,3},{12,8},{14,10},{13,9},{15,11},{20,16},{22,... | collective-permute-start | bytes 786440 | tf_op jit(solution)/shard_map/ppermute | solution.py:146
  47.1 0.7 copy-start.1
  56.5 21.8 %collective-permute-start.5 = (bf16[2,4,128,128]{3,2,1,0:T(8,128)(2,1)}, bf16[2,4,128,128]{3,2,1,0:T(8,128)(2,1)S(1)}, u32[]{:S(2)}, u32[]{:S(2)}) collective-permute-start(bf16[2,4,128,128]{3,2,1,0:T(8,128)(2,1)} %get-tuple-element.18), channel_id=1, source_target_pairs={{6,0},{7,1},{14,8},{15,9},{22,16},{23,17},{30,24},{31,25}} | collective-permute-start | bytes 786440 | tf_op jit(solution)/shard_map/ppermute | solution.py:146
  57.8 20.5 %copy-start.3 = (f32[2,4,128,128]{3,2,1,0:T(8,128)S(1)}, f32[2,4,128,128]{3,2,1,0:T(8,128)}, u32[]{:S(2)}) copy-start(f32[2,4,128,128]{3,2,1,0:T(8,128)} %get-tuple-element.15) | copy-start | bytes 1572868
where the time goes:
time: 80.5 us; the launch traced here: 79.9 us
  Pallas kernels  37.7 us (47%)
  starting transfers between devices  19.7 us (24%)
  waiting for transfers between devices  13.7 us (17%)
  local copies, waits for them, and re-layouts  7.13 us (9%)
  other arithmetic  0.94 us (1%)
    pallas_call x3, Pallas kernels, pair_grads(): pl.pallas_call(functools.partial(pair_kernel, shifts, docs.shape[0], shar...  30.9 us
    ppermute x6, waiting for transfers between devices, moved(): return lax.ppermute(x, 'ctx', pairs)  13.7 us
    ppermute x6, starting transfers between devices, moved(): return lax.ppermute(x, 'ctx', pairs)  13.4 us
    pallas_call x1, Pallas kernels, query_grads(): pl.pallas_call(functools.partial(query_kernel, share), grid=(kv_heads,),...  6.8 us
    all_to_all x1, starting transfers between devices, local(): lax.all_to_all(stats, 'ctx', split_axis=0, concat_axis=0, tiled=True)  6.35 us
    unnamed x12, local copies, waits for them, and re-layouts  3.66 us
  transfers between devices with their start and end apart: 7, of which 2 were waited for; matrix products, arithmetic and copies ran while one was open for 4% of the time, Pallas kernels for 47%

commit v1 on v0

v1 whole, which is shorter than its diff:
```python
import functools

import jax
import jax.numpy as jnp
from jax import lax
from jax.experimental import pallas as pl
from jax.experimental.pallas import tpu as pltpu
from jax.sharding import PartitionSpec as P


DOC_MAX = 384
LOG2E = 1.4426950408889634
MIB = 1024 * 1024
VMEM = pl.BlockSpec(memory_space=pltpu.VMEM)
HBM = pl.BlockSpec(memory_space=pltpu.HBM)


def dot_nt(left, right):
    return lax.dot_general(left, right, (((1,), (1,)), ((), ())), preferred_element_type=jnp.float32)


def dot_nn(left, right):
    return lax.dot_general(left, right, (((1,), (0,)), ((), ())), preferred_element_type=jnp.float32)


def doc_start(docs_ref, token):
    start = jnp.zeros_like(token)
    end = jnp.int32(0)
    for d in range(docs_ref.shape[0]):
        end = end + docs_ref[d]
        start = jnp.where(token >= end, end, start)
    return start


def row_tokens(rows, share, first):
    return first + lax.broadcasted_iota(jnp.int32, (1, rows), 1) // share


def spread_stats(share, in_ref, out_ref):
    kv_heads, _, _, tok = in_ref.shape
    rows = tok * share
    at = lax.broadcasted_iota(jnp.int32, (tok, rows), 1) // share
    spread = (at == lax.broadcasted_iota(jnp.int32, (tok, rows), 0)).astype(jnp.float32)
    spread = spread.astype(jnp.bfloat16)
    head = lax.broadcasted_iota(jnp.int32, (share, rows), 0)
    own = lax.broadcasted_iota(jnp.int32, (share, rows), 1) % share == head
    for i in range(kv_heads):
        x = in_ref[i].reshape(2 * share, tok)
        high = x.astype(jnp.bfloat16)
        rest = x - high.astype(jnp.float32)
        mid = rest.astype(jnp.bfloat16)
        low = (rest - mid.astype(jnp.float32)).astype(jnp.bfloat16)
        y = dot_nn(high, spread) + dot_nn(mid, spread) + dot_nn(low, spread)
        out_ref[i, 0:1] = jnp.sum(jnp.where(own, y[:share], 0.0), axis=0, keepdims=True) * LOG2E
        out_ref[i, 1:2] = jnp.sum(jnp.where(own, y[share:], 0.0), axis=0, keepdims=True)


def tile_grads(k, v, q, g, norm, delta, ok):
    scores = dot_nt(k, q)
    probs = jnp.exp2(scores * (q.shape[1] ** (-0.5) * LOG2E) - norm)
    if ok is not None:
        probs = jnp.where(ok, probs, 0.0)
    ds = (probs * (dot_nt(v, g) - delta)).astype(jnp.bfloat16)
    return ds, dot_nn(ds, q), dot_nn(probs.astype(jnp.bfloat16), g)


def head_rows(ref, i, share, first, count):
    block = ref[pl.ds(first, count), pl.ds(pl.multiple_of(i * share, share), share), :]
    return block.reshape(count * share, ref.shape[2])


def past_kernel(shift, share, start_ref, q_ref, g_ref, stats_ref, kv_ref, ds_ref, out_ref, acc_ref, ready):
    tok, _, dim = q_ref.shape
    _, kv_heads, keys, _ = kv_ref.shape
    scaling = dim ** (-0.5)
    base = (lax.axis_index("ctx") - shift) * keys
    none = (base < 0) | (jnp.min(start_ref[...]) >= base + keys)
    full = jnp.logical_not(none) & (jnp.max(start_ref[...]) <= base)

    @pl.when(full)
    def _():
        for i in range(kv_heads):
            ready(i)
            q = head_rows(q_ref, i, share, 0, tok)
            g = head_rows(g_ref, i, share, 0, tok)
            ds, dk, dv = tile_grads(
                kv_ref[0, i], kv_ref[1, i], q, g, stats_ref[i, 0:1], stats_ref[i, 1:2], None
            )
            ds_ref[i] = ds
            out_ref[0, i] = (dk * scaling).astype(jnp.bfloat16)
            out_ref[1, i] = dv.astype(jnp.bfloat16)

    @pl.when(jnp.logical_not(full))
    def _():
        for i in range(kv_heads):
            ready(i)

    @pl.when(none)
    def _():
        ds_ref[...] = jnp.zeros_like(ds_ref)
        out_ref[...] = jnp.zeros_like(out_ref)

    @pl.when(jnp.logical_not(none | full))
    def _():
        step = 32

        def one_head(i, _):
            acc_ref[...] = jnp.zeros_like(acc_ref)
            for b in range(tok // step):
                cut = slice(b * step * share, (b + 1) * step * share)
                start = start_ref[:, cut]
                reached = jnp.min(start) < base + keys

                @pl.when(reached)
                def _():
                    q = head_rows(q_ref, i, share, b * step, step)
                    g = head_rows(g_ref, i, share, b * step, step)
                    key = base + lax.broadcasted_iota(jnp.int32, (keys, step * share), 0)
                    ds, dk, dv = tile_grads(
                        kv_ref[0, i],
                        kv_ref[1, i],
                        q,
                        g,
                        stats_ref[i, 0:1, cut],
                        stats_ref[i, 1:2, cut],
                        key >= start,
                    )
                    ds_ref[i, :, cut] = ds
                    acc_ref[0] += dk
                    acc_ref[1] += dv

                @pl.when(jnp.logical_not(reached))
                def _():
                    ds_ref[i, :, cut] = jnp.zeros((keys, step * share), jnp.bfloat16)

            out_ref[0, i] = (acc_ref[0] * scaling).astype(jnp.bfloat16)
            out_ref[1, i] = acc_ref[1].astype(jnp.bfloat16)
            return 0

        lax.fori_loop(0, kv_heads, one_head, 0)


def first_past_kernel(share, docs_hbm, q_hbm, g_hbm, raw_ref, kv_ref, *refs):
    ds_ref, out_ref, q_ref, g_ref, stats_ref, start_ref, acc_ref, docs_ref, docs_sem, q_sem, g_sem = refs
    tok = q_ref.shape[0]

    def copies(i):
        heads = pl.ds(i * share, share)
        return (
            pltpu.make_async_copy(q_hbm.at[:, heads, :], q_ref.at[:, heads, :], q_sem.at[i]),
            pltpu.make_async_copy(g_hbm.at[:, heads, :], g_ref.at[:, heads, :], g_sem.at[i]),
        )

    def ready(i):
        for copy in copies(i):
            copy.wait()

    docs_copy = pltpu.make_async_copy(docs_hbm, docs_ref, docs_sem)
    docs_copy.start()
    for i in range(kv_ref.shape[1]):
        for copy in copies(i):
            copy.start()
    spread_stats(share, raw_ref, stats_ref)
    docs_copy.wait()
    token = row_tokens(tok * share, share, lax.axis_index("ctx") * tok)
    start_ref[...] = doc_start(docs_ref, token)
    past_kernel(1, share, start_ref, q_ref, g_ref, stats_ref, kv_ref, ds_ref, out_ref, acc_ref, ready)


def next_past_kernel(shift, share, *refs):
    past_kernel(shift, share, *refs, lambda i: None)


def past_cost(kv, rows):
    _, kv_heads, keys, dim = kv.shape
    return pl.CostEstimate(
        flops=8 * kv_heads * keys * rows * dim,
        transcendentals=kv_heads * keys * rows,
        bytes_accessed=4 * kv_heads * rows * dim,
    )


def first_past(share, docs, q, g, raw, kv):
    _, kv_heads, keys, dim = kv.shape
    rows = q.shape[0] * share
    return pl.pallas_call(
        functools.partial(first_past_kernel, share),
        in_specs=[HBM, HBM, HBM, VMEM, VMEM],
        out_specs=[VMEM] * 6,
        out_shape=[
            jax.ShapeDtypeStruct((kv_heads, keys, rows), jnp.bfloat16),
            jax.ShapeDtypeStruct(kv.shape, jnp.bfloat16),
            jax.ShapeDtypeStruct(q.shape, q.dtype),
            jax.ShapeDtypeStruct(g.shape, g.dtype),
            jax.ShapeDtypeStruct((kv_heads, 2, rows), jnp.float32),
            jax.ShapeDtypeStruct((1, rows), jnp.int32),
        ],
        scratch_shapes=[
            pltpu.VMEM((2, keys, dim), jnp.float32),
            pltpu.SMEM(docs.shape, jnp.int32),
            pltpu.SemaphoreType.DMA,
            pltpu.SemaphoreType.DMA((kv_heads,)),
            pltpu.SemaphoreType.DMA((kv_heads,)),
        ],
        compiler_params=pltpu.CompilerParams(vmem_limit_bytes=47 * MIB),
        cost_estimate=past_cost(kv, rows),
        name="past_1",
    )(docs, q, g, raw, kv)


def next_past(shift, share, start, q, g, stats, kv):
    _, kv_heads, keys, dim = kv.shape
    rows = stats.shape[2]
    return pl.pallas_call(
        functools.partial(next_past_kernel, shift, share),
        in_specs=[VMEM] * 5,
        out_specs=[VMEM, VMEM],
        out_shape=[
            jax.ShapeDtypeStruct((kv_heads, keys, rows), jnp.bfloat16),
            jax.ShapeDtypeStruct(kv.shape, jnp.bfloat16),
        ],
        scratch_shapes=[pltpu.VMEM((2, keys, dim), jnp.float32)],
        compiler_params=pltpu.CompilerParams(vmem_limit_bytes=24 * MIB),
        cost_estimate=past_cost(kv, rows),
    )(start, q, g, stats, kv)


def last_kernel(share, start_ref, q_ref, g_ref, stats_ref, kv_ref, *refs):
    n = (len(refs) - 2) // 2
    past_kv, past_ds, (dq_ref, out_ref) = refs[:n], refs[n : 2 * n], refs[2 * n :]
    tok, _, dim = q_ref.shape
    _, kv_heads, keys, _ = kv_ref.shape
    rows = tok * share
    scaling = dim ** (-0.5)
    first = lax.axis_index("ctx") * tok
    key = first + lax.broadcasted_iota(jnp.int32, (keys, rows), 0)
    ok = (key >= start_ref[...]) & (key <= row_tokens(rows, share, first))
    for i in range(kv_heads):
        k = kv_ref[0, i]
        q = head_rows(q_ref, i, share, 0, tok)
        g = head_rows(g_ref, i, share, 0, tok)
        ds, dk, dv = tile_grads(k, kv_ref[1, i], q, g, stats_ref[i, 0:1], stats_ref[i, 1:2], ok)
        out_ref[0, i] = dk * scaling
        out_ref[1, i] = dv
        ks = jnp.concatenate([k] + [r[0, i] for r in past_kv], axis=0)
        ds = jnp.concatenate([ds] + [r[i] for r in past_ds], axis=0)
        dq = dot_nn(ks.T, ds) * scaling
        dq_ref[:, i * share : (i + 1) * share, :] = dq.T.astype(jnp.bfloat16).reshape(tok, share, dim)


def last_grads(share, start, q, g, stats, kvs, ds_list):
    _, kv_heads, keys, dim = kvs[0].shape
    rows = stats.shape[2]
    n = len(kvs)
    return pl.pallas_call(
        functools.partial(last_kernel, share),
        in_specs=[VMEM] * (4 + n + len(ds_list)),
        out_specs=[VMEM, VMEM],
        out_shape=[
            jax.ShapeDtypeStruct(q.shape, jnp.bfloat16),
            jax.ShapeDtypeStruct(kvs[0].shape, jnp.float32),
        ],
        compiler_params=pltpu.CompilerParams(vmem_limit_bytes=24 * MIB),
        cost_estimate=pl.CostEstimate(
            flops=(8 + 2 * n) * kv_heads * keys * rows * dim,
            transcendentals=kv_heads * keys * rows,
            bytes_accessed=4 * kv_heads * rows * dim,
        ),
        name="last",
    )(start, q, g, stats, *kvs, *ds_list)


def local(query_rows, key_rows, value_rows, out_grad, softmax_delta, log_norm, doc_lengths):
    groups = lax.axis_size("ctx")
    tok, heads, _ = query_rows.shape
    kv_heads = key_rows.shape[1]
    share = heads // kv_heads
    per_dev = heads // groups
    reach = min(groups - 1, -(-(DOC_MAX - 1) // tok))

    def moved(x, s):
        pairs = [(i, i + s) for i in range(groups) if 0 <= i + s < groups]
        return lax.ppermute(x, "ctx", pairs)

    kvs = [jnp.stack([key_rows, value_rows]).transpose(0, 2, 1, 3)]
    for _ in range(1, reach + 1):
        kvs.append(moved(kvs[-1], 1))
    raw = jnp.stack([log_norm[0], softmax_delta[0]])
    raw = raw.reshape(2, per_dev, groups, tok).transpose(2, 0, 1, 3)
    raw = lax.all_to_all(raw, "ctx", split_axis=0, concat_axis=0, tiled=True)
    raw = raw.reshape(kv_heads, groups // kv_heads, 2, per_dev, tok)
    raw = raw.transpose(0, 2, 1, 3, 4).reshape(kv_heads, 2, share, tok)
    ds, part, q, g, stats, start = first_past(share, doc_lengths, query_rows, out_grad, raw, kvs[1])
    terms = [moved(part, -1)]
    ds_list = [ds]
    for s in range(2, reach + 1):
        ds, part = next_past(s, share, start, q, g, stats, kvs[s])
        ds_list.append(ds)
        terms.append(moved(part, -s))
    query_grad, total = last_grads(share, start, q, g, stats, kvs, ds_list)
    for term in terms:
        total = total + term.astype(jnp.float32)
    total = total.astype(jnp.bfloat16).transpose(0, 2, 1, 3)
    return (query_grad, total[0], total[1])


def solution(mesh):
    rows = P(("dp", "ctx"), "tp", None)
    stats = P("tp", "ctx", "dp")
    return jax.shard_map(
        local,
        mesh=mesh,
        in_specs=(rows, rows, rows, rows, stats, stats, P("dp")),
        out_specs=(rows, rows, rows),
        check_vma=False,
    )
```

time: 80.5 us -> 60.2 us (0.75)
  Pallas kernels: 37.7 us -> 8.98 us
  waiting for transfers between devices: 13.7 us -> 24.1 us
  local copies, waits for them, and re-layouts: 7.13 us -> 3.2 us
  starting transfers between devices: 19.7 us -> 21.3 us
    pallas_call x4, Pallas kernels: 37.7 us -> 8.98 us  [the longest x1 5.48 us: last_grads(): pl.pallas_call(functools.partial(last_kernel, share), in_specs=[VMEM] * (...]
    ppermute x6, waiting for transfers between devices: 13.7 us -> 22.5 us  [moved(): return lax.ppermute(x, 'ctx', pairs)]
    ppermute x6, starting transfers between devices: 13.4 us -> 17.4 us  [moved(): return lax.ppermute(x, 'ctx', pairs)]
    all_to_all x1, starting transfers between devices: 6.35 us -> 3.85 us  [local(): raw = lax.all_to_all(raw, 'ctx', split_axis=0, concat_axis=0, tiled=True)]
    squeeze x2 -> x0, local copies, waits for them, and re-layouts: 1.54 us -> none  [local(): norm, delta = (stats[0], stats[1])]
    all_to_all x1, waiting for transfers between devices: 0.01 us -> 1.53 us  [local(): raw = lax.all_to_all(raw, 'ctx', split_axis=0, concat_axis=0, tiled=True)]
    unnamed x12 -> x4, local copies, waits for them, and re-layouts: 3.66 us -> 2.17 us
    transpose x1 -> x2, other arithmetic: 0.03 us -> 1.44 us  [the longest x1 1.41 us: local(): raw = raw.reshape(2, per_dev, groups, tok).transpose(2, 0, 1, 3)]
  transfers between devices with their start and end apart: 7 -> 7, of which waited for: 2 -> 3; matrix products, arithmetic and copies ran while one was open for 4% -> 2% of each run, Pallas kernels for 47% -> 15%
where the time goes in v1:
time: 60.2 us; the launch traced here: 59.8 us
  waiting for transfers between devices  24.1 us (40%)
  starting transfers between devices  21.3 us (35%)
  Pallas kernels  8.98 us (15%)
  local copies, waits for them, and re-layouts  3.2 us (5%)
  other arithmetic  1.57 us (3%)
  between operations  0.74 us (1%)
    ppermute x6, waiting for transfers between devices, moved(): return lax.ppermute(x, 'ctx', pairs)  22.5 us
    ppermute x6, starting transfers between devices, moved(): return lax.ppermute(x, 'ctx', pairs)  17.4 us
    pallas_call x1, Pallas kernels, last_grads(): pl.pallas_call(functools.partial(last_kernel, share), in_specs=[VMEM] * (...  5.48 us
    all_to_all x1, starting transfers between devices, local(): raw = lax.all_to_all(raw, 'ctx', split_axis=0, concat_axis=0, tiled=True)  3.85 us
    pallas_call x1, Pallas kernels, first_past(): pl.pallas_call(functools.partial(first_past_kernel, share), in_specs=[HBM...  2.53 us
    unnamed x4, local copies, waits for them, and re-layouts  2.17 us
    all_to_all x1, waiting for transfers between devices, local(): raw = lax.all_to_all(raw, 'ctx', split_axis=0, concat_axis=0, tiled=True)  1.53 us
    transpose x1, other arithmetic, local(): raw = raw.reshape(2, per_dev, groups, tok).transpose(2, 0, 1, 3)  1.41 us
  transfers between devices with their start and end apart: 7, of which 3 were waited for; matrix products, arithmetic and copies ran while one was open for 2% of the time, Pallas kernels for 15%

profile of v1, /device:TPU:0, one launch (start us, length us, event | category | flops | bytes accessed | tf_op | source)
XLA Modules:
  0.0 59.8 jit_solution(10709484654669646990)
XLA Ops:
  0.6 1.0 %copy_bitcast_fusion = (bf16[1,128,4,128]{3,1,2,0:T(8,128)(2,1)S(1)}, bf16[1,128,4,128]{3,1,2,0:T(8,128)(2,1)S(1)}) fusion(bf16[128,4,128]{2,1,0:T(4,128)(2,1)} %param.9, bf16[128,4,128]{2,1,0:T(4,128)(2,1)} %param.8), kind=kLoop, calls=%fused_computation.5 | loop fusion | bytes 524288 | tf_op jit(solution)/shard_map/stack | solution.py:285
  1.7 5.0 %collective-permute-start = (bf16[2,4,128,128]{3,2,1,0:T(8,128)(2,1)S(1)}, bf16[2,4,128,128]{3,2,1,0:T(8,128)(2,1)S(1)}, u32[]{:S(2)}, u32[]{:S(2)}) collective-permute-start(bf16[2,4,128,128]{3,2,1,0:T(8,128)(2,1)S(1)} %maximum_bitcast_fusion.kv_ref), channel_id=1, source_target_pairs={{0,2},{2,4},{4,6},{1,3},{3,5},{5,7},{8,10},{10,12},{12,14},{9,11},... | collective-permute-start | bytes 786440 | tf_op jit(solution)/shard_map/ppermute | solution.py:283
  6.7 5.5 %collective-permute-done.kv_ref.refs_0_ = bf16[2,4,128,128]{3,2,1,0:T(8,128)(2,1)S(1)} collective-permute-done((bf16[2,4,128,128]{3,2,1,0:T(8,128)(2,1)S(1)}, bf16[2,4,128,128]{3,2,1,0:T(8,128)(2,1)S(1)}, u32[]{:S(2)}, u32[]{:S(2)}) %collective-permute-start) | collective-permute-done | bytes 262176 | tf_op jit(solution)/shard_map/ppermute | solution.py:283
  12.2 4.4 %collective-permute-start.1 = (bf16[2,4,128,128]{3,2,1,0:T(8,128)(2,1)S(1)}, bf16[2,4,128,128]{3,2,1,0:T(8,128)(2,1)S(1)}, u32[]{:S(2)}, u32[]{:S(2)}) collective-permute-start(bf16[2,4,128,128]{3,2,1,0:T(8,128)(2,1)S(1)} %collective-permute-done.kv_ref.refs_0_), channel_id=1, source_target_pairs={{0,2},{2,4},{4,6},{1,3},{3,5},{5,7},{8,10},{10,12},{12,14},{9,11},... | collective-permute-start | bytes 786440 | tf_op jit(solution)/shard_map/ppermute | solution.py:283
  16.6 1.4 %bitcast_bitcast_fusion = f32[4,2,16,128]{3,2,1,0:T(8,128)} fusion(f32[1,16,512]{2,1,0:T(8,128)} %param.11, f32[1,16,512]{2,1,0:T(8,128)} %param.12), kind=kLoop, calls=%fused_computation.7 | loop fusion | flops 16384 | bytes 131072 | tf_op jit(solution)/shard_map/transpose | solution.py:289
  18.0 3.8 %all-to-all-start = ((f32[4,2,16,128]{3,2,1,0:T(8,128)}), f32[4,2,16,128]{3,2,1,0:T(8,128)S(1)}, u32[]{:S(2)}, u32[]{:S(2)}) async-start(f32[4,2,16,128]{3,2,1,0:T(8,128)} %bitcast_bitcast_fusion), calls=%async_computation | async-start | bytes 131072 | tf_op jit(solution)/shard_map/all_to_all | solution.py:290
  21.8 0.0 collective-permute-done.1.refs_4_.refs_1_
  21.8 4.2 %collective-permute-start.2 = (bf16[2,4,128,128]{3,2,1,0:T(8,128)(2,1)S(1)}, bf16[2,4,128,128]{3,2,1,0:T(8,128)(2,1)S(1)}, u32[]{:S(2)}, u32[]{:S(2)}) collective-permute-start(bf16[2,4,128,128]{3,2,1,0:T(8,128)(2,1)S(1)} %collective-permute-done.1.refs_4_.refs_1_), channel_id=1, source_target_pairs={{0,2},{2,4},{4,6},{1,3},{3,5},{5,7},{8,10},{10,12},{12,14},{9,11},... | collective-permute-start | bytes 786440 | tf_op jit(solution)/shard_map/ppermute | solution.py:283
  26.1 1.5 %all-to-all-done.raw_ref = f32[4,2,16,128]{3,2,1,0:T(8,128)S(1)} async-done(((f32[4,2,16,128]{3,2,1,0:T(8,128)}), f32[4,2,16,128]{3,2,1,0:T(8,128)S(1)}, u32[]{:S(2)}, u32[]{:S(2)}) %all-to-all-start) | async-done | bytes 65568 | tf_op jit(solution)/shard_map/all_to_all | solution.py:290
  27.6 0.0 copy-start
  27.6 0.7 %copy-done = s32[3]{0:T(128)S(1)} copy-done((s32[3]{0:T(128)S(1)}, s32[3]{0:T(128)}, u32[]{:S(2)}) %copy-start) | copy-done | bytes 36
  28.2 2.5 %past_1.1 = (bf16[4,128,2048]{2,1,0:T(8,128)(2,1)S(1)}, bf16[2,4,128,128]{3,2,1,0:T(8,128)(2,1)S(1)}, bf16[128,64,128]{2,1,0:T(8,128)(2,1)S(1)}, bf16[128,64,128...) custom-call(s32[3]{0:T(128)S(1)} %copy-done, bf16[128,64,128]{2,1,0:T(8,128)(2,1)} %q_hbm.1, ...), custom_call_target="tpu_custom_call" | custom-call | flops 1073741824 | bytes 4194304 | tf_op jit(solution)/shard_map/past_1/pallas_call | solution.py:186
  30.8 1.3 %collective-permute-start.3 = (bf16[2,4,128,128]{3,2,1,0:T(8,128)(2,1)S(1)}, bf16[2,4,128,128]{3,2,1,0:T(8,128)(2,1)S(1)}, u32[]{:S(2)}, u32[]{:S(2)}) collective-permute-start(bf16[2,4,128,128]{3,2,1,0:T(8,128)(2,1)S(1)} %get-tuple-element.24), channel_id=1, source_target_pairs={{2,0},{4,2},{6,4},{3,1},{5,3},{7,5},{10,8},{12,10},{14,12},{11,9},... | collective-permute-start | bytes 786440 | tf_op jit(solution)/shard_map/ppermute | solution.py:283
  32.1 0.4 shard_map.94
  32.5 1.3 %collective-permute-start.4 = (bf16[2,4,128,128]{3,2,1,0:T(8,128)(2,1)S(1)}, bf16[2,4,128,128]{3,2,1,0:T(8,128)(2,1)S(1)}, u32[]{:S(2)}, u32[]{:S(2)}) collective-permute-start(bf16[2,4,128,128]{3,2,1,0:T(8,128)(2,1)S(1)} %get-tuple-element.25), channel_id=1, source_target_pairs={{4,0},{6,2},{5,1},{7,3},{12,8},{14,10},{13,9},{15,11},{20,16},{22,... | collective-permute-start | bytes 786440 | tf_op jit(solution)/shard_map/ppermute | solution.py:283
  33.8 0.0 collective-permute-done.2.refs_4_.refs_2_
  33.8 0.6 shard_map.95
  34.4 1.3 %collective-permute-start.5 = (bf16[2,4,128,128]{3,2,1,0:T(8,128)(2,1)S(1)}, bf16[2,4,128,128]{3,2,1,0:T(8,128)(2,1)S(1)}, u32[]{:S(2)}, u32[]{:S(2)}) collective-permute-start(bf16[2,4,128,128]{3,2,1,0:T(8,128)(2,1)S(1)} %get-tuple-element.26), channel_id=1, source_target_pairs={{6,0},{7,1},{14,8},{15,9},{22,16},{23,17},{30,24},{31,25}} | collective-permute-start | bytes 786440 | tf_op jit(solution)/shard_map/ppermute | solution.py:283
  35.7 5.5 %last.1 = (bf16[128,64,128]{2,1,0:T(8,128)(2,1)}, f32[2,4,128,128]{3,2,1,0:T(8,128)S(1)}) custom-call(s32[1,2048]{1,0:T(1,128)S(1)} %get-tuple-element.15.refs_0_.start_ref, bf16[128,64,128]{2,1,0:T(8,128)(2,1)S(1)} %get-tuple-element.16.refs_1_.q_ref, bf16[128,64,128]{2,1,0:T(8,128)(2,1)S(1)} %get-tuple-element.17.refs_2_.g_ref, ...), custom_call_target="tpu_custom_call" | custom-call | flops 2147483648 | bytes 4194304 | tf_op jit(solution)/shard_map/last/pallas_call | solution.py:255
  41.2 0.0 collective-permute-done.3
  41.2 17.0 %collective-permute-done.4 = bf16[2,4,128,128]{3,2,1,0:T(8,128)(2,1)S(1)} collective-permute-done((bf16[2,4,128,128]{3,2,1,0:T(8,128)(2,1)S(1)}, bf16[2,4,128,128]{3,2,1,0:T(8,128)(2,1)S(1)}, u32[]{:S(2)}, u32[]{:S(2)}) %collective-permute-start.4) | collective-permute-done | bytes 262176 | tf_op jit(solution)/shard_map/ppermute | solution.py:283
  58.1 0.0 collective-permute-done.5
  58.1 0.1 fusion
  58.3 0.8 %copy.18 = bf16[128,4,128]{2,1,0:T(4,128)(2,1)} copy(bf16[128,4,128]{2,0,1:T(8,128)(2,1)S(1)} %get-tuple-element.33) | data formatting | bytes 262144
  59.1 0.8 %copy.17 = bf16[128,4,128]{2,1,0:T(4,128)(2,1)} copy(bf16[128,4,128]{2,0,1:T(8,128)(2,1)S(1)} %get-tuple-element.34) | data formatting | bytes 262144
  (2 shorter events, 0.0 us)
Async XLA Ops:
  1.7 10.5 %collective-permute-start = (bf16[2,4,128,128]{3,2,1,0:T(8,128)(2,1)S(1)}, bf16[2,4,128,128]{3,2,1,0:T(8,128)(2,1)S(1)}, u32[]{:S(2)}, u32[]{:S(2)}) collective-permute-start(bf16[2,4,128,128]{3,2,1,0:T(8,128)(2,1)S(1)} %maximum_bitcast_fusion.kv_ref), channel_id=1, source_target_pairs={{0,2},{2,4},{4,6},{1,3},{3,5},{5,7},{8,10},{10,12},{12,14},{9,11},... | collective-permute-start | bytes 786440 | tf_op jit(solution)/shard_map/ppermute | solution.py:283
  12.2 9.7 %collective-permute-start.1 = (bf16[2,4,128,128]{3,2,1,0:T(8,128)(2,1)S(1)}, bf16[2,4,128,128]{3,2,1,0:T(8,128)(2,1)S(1)}, u32[]{:S(2)}, u32[]{:S(2)}) collective-permute-start(bf16[2,4,128,128]{3,2,1,0:T(8,128)(2,1)S(1)} %collective-permute-done.kv_ref.refs_0_), channel_id=1, source_target_pairs={{0,2},{2,4},{4,6},{1,3},{3,5},{5,7},{8,10},{10,12},{12,14},{9,11},... | collective-permute-start | bytes 786440 | tf_op jit(solution)/shard_map/ppermute | solution.py:283
  18.0 9.6 %all-to-all-start = ((f32[4,2,16,128]{3,2,1,0:T(8,128)}), f32[4,2,16,128]{3,2,1,0:T(8,128)S(1)}, u32[]{:S(2)}, u32[]{:S(2)}) async-start(f32[4,2,16,128]{3,2,1,0:T(8,128)} %bitcast_bitcast_fusion), calls=%async_computation | async-start | bytes 131072 | tf_op jit(solution)/shard_map/all_to_all | solution.py:290
  21.8 11.9 %collective-permute-start.2 = (bf16[2,4,128,128]{3,2,1,0:T(8,128)(2,1)S(1)}, bf16[2,4,128,128]{3,2,1,0:T(8,128)(2,1)S(1)}, u32[]{:S(2)}, u32[]{:S(2)}) collective-permute-start(bf16[2,4,128,128]{3,2,1,0:T(8,128)(2,1)S(1)} %collective-permute-done.1.refs_4_.refs_1_), channel_id=1, source_target_pairs={{0,2},{2,4},{4,6},{1,3},{3,5},{5,7},{8,10},{10,12},{12,14},{9,11},... | collective-permute-start | bytes 786440 | tf_op jit(solution)/shard_map/ppermute | solution.py:283
  27.6 0.7 %copy-start = (s32[3]{0:T(128)S(1)}, s32[3]{0:T(128)}, u32[]{:S(2)}) copy-start(s32[3]{0:T(128)} %docs_hbm.1) | copy-start | bytes 40
  30.8 10.4 %collective-permute-start.3 = (bf16[2,4,128,128]{3,2,1,0:T(8,128)(2,1)S(1)}, bf16[2,4,128,128]{3,2,1,0:T(8,128)(2,1)S(1)}, u32[]{:S(2)}, u32[]{:S(2)}) collective-permute-start(bf16[2,4,128,128]{3,2,1,0:T(8,128)(2,1)S(1)} %get-tuple-element.24), channel_id=1, source_target_pairs={{2,0},{4,2},{6,4},{3,1},{5,3},{7,5},{10,8},{12,10},{14,12},{11,9},... | collective-permute-start | bytes 786440 | tf_op jit(solution)/shard_map/ppermute | solution.py:283
  32.5 25.6 %collective-permute-start.4 = (bf16[2,4,128,128]{3,2,1,0:T(8,128)(2,1)S(1)}, bf16[2,4,128,128]{3,2,1,0:T(8,128)(2,1)S(1)}, u32[]{:S(2)}, u32[]{:S(2)}) collective-permute-start(bf16[2,4,128,128]{3,2,1,0:T(8,128)(2,1)S(1)} %get-tuple-element.25), channel_id=1, source_target_pairs={{4,0},{6,2},{5,1},{7,3},{12,8},{14,10},{13,9},{15,11},{20,16},{22,... | collective-permute-start | bytes 786440 | tf_op jit(solution)/shard_map/ppermute | solution.py:283
  34.4 23.8 %collective-permute-start.5 = (bf16[2,4,128,128]{3,2,1,0:T(8,128)(2,1)S(1)}, bf16[2,4,128,128]{3,2,1,0:T(8,128)(2,1)S(1)}, u32[]{:S(2)}, u32[]{:S(2)}) collective-permute-start(bf16[2,4,128,128]{3,2,1,0:T(8,128)(2,1)S(1)} %get-tuple-element.26), channel_id=1, source_target_pairs={{6,0},{7,1},{14,8},{15,9},{22,16},{23,17},{30,24},{31,25}} | collective-permute-start | bytes 786440 | tf_op jit(solution)/shard_map/ppermute | solution.py:283

commit v2 on v1

--- a/solution.py
+++ b/solution.py
@@ -39,20 +39,23 @@
 def spread_stats(share, in_ref, out_ref):
     kv_heads, _, _, tok = in_ref.shape
     rows = tok * share
+    x = in_ref[...].reshape(kv_heads * 2 * share, tok)
+    high = x.astype(jnp.bfloat16)
+    rest = x - high.astype(jnp.float32)
+    mid = rest.astype(jnp.bfloat16)
+    low = (rest - mid.astype(jnp.float32)).astype(jnp.bfloat16)
     at = lax.broadcasted_iota(jnp.int32, (tok, rows), 1) // share
     spread = (at == lax.broadcasted_iota(jnp.int32, (tok, rows), 0)).astype(jnp.float32)
     spread = spread.astype(jnp.bfloat16)
-    head = lax.broadcasted_iota(jnp.int32, (share, rows), 0)
-    own = lax.broadcasted_iota(jnp.int32, (share, rows), 1) % share == head
+    parts = jnp.concatenate([high, mid, low], axis=1)
+    y = dot_nn(parts, jnp.concatenate([spread] * 3, axis=0))
+    own = lax.broadcasted_iota(jnp.int32, (share, rows), 1) % share
+    own = own == lax.broadcasted_iota(jnp.int32, (share, rows), 0)
     for i in range(kv_heads):
-        x = in_ref[i].reshape(2 * share, tok)
-        high = x.astype(jnp.bfloat16)
-        rest = x - high.astype(jnp.float32)
-        mid = rest.astype(jnp.bfloat16)
-        low = (rest - mid.astype(jnp.float32)).astype(jnp.bfloat16)
-        y = dot_nn(high, spread) + dot_nn(mid, spread) + dot_nn(low, spread)
-        out_ref[i, 0:1] = jnp.sum(jnp.where(own, y[:share], 0.0), axis=0, keepdims=True) * LOG2E
-        out_ref[i, 1:2] = jnp.sum(jnp.where(own, y[share:], 0.0), axis=0, keepdims=True)
+        for j, factor in ((0, LOG2E), (1, 1.0)):
+            first = (2 * i + j) * share
+            row = jnp.sum(jnp.where(own, y[first : first + share], 0.0), axis=0, keepdims=True)
+            out_ref[i, j : j + 1] = row * factor
 
 
 def tile_grads(k, v, q, g, norm, delta, ok):
@@ -270,6 +273,26 @@
     )(start, q, g, stats, *kvs, *ds_list)
 
 
+def sum_kernel(*refs):
+    own_ref, terms, (key_ref, value_ref) = refs[0], refs[1:-2], refs[-2:]
+    for j, ref in enumerate((key_ref, value_ref)):
+        total = own_ref[j]
+        for term in terms:
+            total = total + term[j].astype(jnp.float32)
+        ref[...] = jnp.swapaxes(total, 0, 1).astype(jnp.bfloat16)
+
+
+def sum_terms(own, terms):
+    _, kv_heads, keys, dim = own.shape
+    return pl.pallas_call(
+        sum_kernel,
+        in_specs=[VMEM] * (1 + len(terms)),
+        out_shape=[jax.ShapeDtypeStruct((keys, kv_heads, dim), jnp.bfloat16)] * 2,
+        compiler_params=pltpu.CompilerParams(vmem_limit_bytes=24 * MIB),
+        name="sum",
+    )(own, *terms)
+
+
 def local(query_rows, key_rows, value_rows, out_grad, softmax_delta, log_norm, doc_lengths):
     groups = lax.axis_size("ctx")
     tok, heads, _ = query_rows.shape
@@ -290,7 +313,8 @@
     raw = lax.all_to_all(raw, "ctx", split_axis=0, concat_axis=0, tiled=True)
     raw = raw.reshape(kv_heads, groups // kv_heads, 2, per_dev, tok)
     raw = raw.transpose(0, 2, 1, 3, 4).reshape(kv_heads, 2, share, tok)
-    ds, part, q, g, stats, start = first_past(share, doc_lengths, query_rows, out_grad, raw, kvs[1])
+    docs = jnp.maximum(doc_lengths, 1)
+    ds, part, q, g, stats, start = first_past(share, docs, query_rows, out_grad, raw, kvs[1])
     terms = [moved(part, -1)]
     ds_list = [ds]
     for s in range(2, reach + 1):
@@ -298,10 +322,8 @@
         ds_list.append(ds)
         terms.append(moved(part, -s))
     query_grad, total = last_grads(share, start, q, g, stats, kvs, ds_list)
-    for term in terms:
-        total = total + term.astype(jnp.float32)
-    total = total.astype(jnp.bfloat16).transpose(0, 2, 1, 3)
-    return (query_grad, total[0], total[1])
+    key_grad, value_grad = sum_terms(total, terms)
+    return (query_grad, key_grad, value_grad)
 
 
 def solution(mesh):

time: 60.2 us -> 58.8 us (0.977)
  local copies, waits for them, and re-layouts: 3.2 us -> 1 us
  Pallas kernels: 8.98 us -> 9.79 us
    unnamed x4 -> x0, local copies, waits for them, and re-layouts: 2.17 us -> none
    pallas_call x0 -> x1, Pallas kernels: none -> 0.89 us  [sum_terms(): pl.pallas_call(sum_kernel, in_specs=[VMEM] * (1 + len(terms)), out_shape=...]
    all_to_all x1, waiting for transfers between devices: 1.53 us -> 0.87 us  [local(): raw = lax.all_to_all(raw, 'ctx', split_axis=0, concat_axis=0, tiled=True)]
    max x0 -> x1, other arithmetic: none -> 0.66 us  [local(): docs = jnp.maximum(doc_lengths, 1)]
  transfers between devices with their start and end apart: 7 -> 7, of which waited for: 3 -> 3; matrix products, arithmetic and copies ran while one was open for 2% -> 4% of each run, Pallas kernels for 15% -> 15%
where the time goes in v2:
time: 58.8 us; the launch traced here: 58.4 us
  waiting for transfers between devices  23.5 us (40%)
  starting transfers between devices  21.3 us (36%)
  Pallas kernels  9.79 us (17%)
  other arithmetic  2.1 us (4%)
  local copies, waits for them, and re-layouts  1 us (2%)
  between operations  0.73 us (1%)
    ppermute x6, waiting for transfers between devices, moved(): return lax.ppermute(x, 'ctx', pairs)  22.6 us
    ppermute x6, starting transfers between devices, moved(): return lax.ppermute(x, 'ctx', pairs)  17.4 us
    pallas_call x1, Pallas kernels, last_grads(): pl.pallas_call(functools.partial(last_kernel, share), in_specs=[VMEM] * (...  5.47 us
    all_to_all x1, starting transfers between devices, local(): raw = lax.all_to_all(raw, 'ctx', split_axis=0, concat_axis=0, tiled=True)  3.85 us
    pallas_call x1, Pallas kernels, first_past(): pl.pallas_call(functools.partial(first_past_kernel, share), in_specs=[HBM...  2.46 us
    transpose x1, other arithmetic, local(): raw = raw.reshape(2, per_dev, groups, tok).transpose(2, 0, 1, 3)  1.41 us
  transfers between devices with their start and end apart: 7, of which 3 were waited for; matrix products, arithmetic and copies ran while one was open for 4% of the time, Pallas kernels for 15%

profile of v2, /device:TPU:0, one launch (start us, length us, event | category | flops | bytes accessed | tf_op | source)
XLA Modules:
  0.0 58.4 jit_solution(1293466635995889975)
XLA Ops:
  0.6 1.0 %copy_bitcast_fusion = (bf16[1,128,4,128]{3,1,2,0:T(8,128)(2,1)S(1)}, bf16[1,128,4,128]{3,1,2,0:T(8,128)(2,1)S(1)}) fusion(bf16[128,4,128]{2,1,0:T(4,128)(2,1)} %param.9, bf16[128,4,128]{2,1,0:T(4,128)(2,1)} %param.8), kind=kLoop, calls=%fused_computation.1 | loop fusion | bytes 524288 | tf_op jit(solution)/shard_map/stack | solution.py:308
  1.7 5.0 %collective-permute-start = (bf16[2,4,128,128]{3,2,1,0:T(8,128)(2,1)S(1)}, bf16[2,4,128,128]{3,2,1,0:T(8,128)(2,1)S(1)}, u32[]{:S(2)}, u32[]{:S(2)}) collective-permute-start(bf16[2,4,128,128]{3,2,1,0:T(8,128)(2,1)S(1)} %maximum_bitcast_fusion.kv_ref), channel_id=1, source_target_pairs={{0,2},{2,4},{4,6},{1,3},{3,5},{5,7},{8,10},{10,12},{12,14},{9,11},... | collective-permute-start | bytes 786440 | tf_op jit(solution)/shard_map/ppermute | solution.py:306
  6.7 5.5 %collective-permute-done.kv_ref.refs_0_ = bf16[2,4,128,128]{3,2,1,0:T(8,128)(2,1)S(1)} collective-permute-done((bf16[2,4,128,128]{3,2,1,0:T(8,128)(2,1)S(1)}, bf16[2,4,128,128]{3,2,1,0:T(8,128)(2,1)S(1)}, u32[]{:S(2)}, u32[]{:S(2)}) %collective-permute-start) | collective-permute-done | bytes 262176 | tf_op jit(solution)/shard_map/ppermute | solution.py:306
  12.2 4.4 %collective-permute-start.1 = (bf16[2,4,128,128]{3,2,1,0:T(8,128)(2,1)S(1)}, bf16[2,4,128,128]{3,2,1,0:T(8,128)(2,1)S(1)}, u32[]{:S(2)}, u32[]{:S(2)}) collective-permute-start(bf16[2,4,128,128]{3,2,1,0:T(8,128)(2,1)S(1)} %collective-permute-done.kv_ref.refs_0_), channel_id=1, source_target_pairs={{0,2},{2,4},{4,6},{1,3},{3,5},{5,7},{8,10},{10,12},{12,14},{9,11},... | collective-permute-start | bytes 786440 | tf_op jit(solution)/shard_map/ppermute | solution.py:306
  16.6 1.4 %bitcast_bitcast_fusion = f32[4,2,16,128]{3,2,1,0:T(8,128)} fusion(f32[1,16,512]{2,1,0:T(8,128)} %param.11, f32[1,16,512]{2,1,0:T(8,128)} %param.12), kind=kLoop, calls=%fused_computation.3 | loop fusion | flops 16384 | bytes 131072 | tf_op jit(solution)/shard_map/transpose | solution.py:312
  18.0 3.8 %all-to-all-start = ((f32[4,2,16,128]{3,2,1,0:T(8,128)}), f32[4,2,16,128]{3,2,1,0:T(8,128)S(1)}, u32[]{:S(2)}, u32[]{:S(2)}) async-start(f32[4,2,16,128]{3,2,1,0:T(8,128)} %bitcast_bitcast_fusion), calls=%async_computation | async-start | bytes 131072 | tf_op jit(solution)/shard_map/all_to_all | solution.py:313
  21.8 0.0 collective-permute-done.1.refs_4_.refs_1_
  21.8 4.2 %collective-permute-start.2 = (bf16[2,4,128,128]{3,2,1,0:T(8,128)(2,1)S(1)}, bf16[2,4,128,128]{3,2,1,0:T(8,128)(2,1)S(1)}, u32[]{:S(2)}, u32[]{:S(2)}) collective-permute-start(bf16[2,4,128,128]{3,2,1,0:T(8,128)(2,1)S(1)} %collective-permute-done.1.refs_4_.refs_1_), channel_id=1, source_target_pairs={{0,2},{2,4},{4,6},{1,3},{3,5},{5,7},{8,10},{10,12},{12,14},{9,11},... | collective-permute-start | bytes 786440 | tf_op jit(solution)/shard_map/ppermute | solution.py:306
  26.1 0.7 %broadcast_maximum_fusion.docs_hbm = s32[3]{0:T(128)S(1)} fusion(s32[3]{0:T(128)} %param.13), kind=kLoop, calls=%fused_computation.5 | loop fusion | flops 3 | bytes 24 | tf_op jit(solution)/shard_map/max | solution.py:316
  26.7 0.9 %all-to-all-done.raw_ref = f32[4,2,16,128]{3,2,1,0:T(8,128)S(1)} async-done(((f32[4,2,16,128]{3,2,1,0:T(8,128)}), f32[4,2,16,128]{3,2,1,0:T(8,128)S(1)}, u32[]{:S(2)}, u32[]{:S(2)}) %all-to-all-start) | async-done | bytes 65568 | tf_op jit(solution)/shard_map/all_to_all | solution.py:313
  27.6 2.5 %past_1.1 = (bf16[4,128,2048]{2,1,0:T(8,128)(2,1)S(1)}, bf16[2,4,128,128]{3,2,1,0:T(8,128)(2,1)S(1)}, bf16[128,64,128]{2,1,0:T(8,128)(2,1)S(1)}, bf16[128,64,128...) custom-call(s32[3]{0:T(128)S(1)} %broadcast_maximum_fusion.docs_hbm, ...), custom_call_target="tpu_custom_call" | custom-call | flops 1073741824 | bytes 4194304 | tf_op jit(solution)/shard_map/past_1/pallas_call | solution.py:189
  30.1 1.3 %collective-permute-start.3 = (bf16[2,4,128,128]{3,2,1,0:T(8,128)(2,1)S(1)}, bf16[2,4,128,128]{3,2,1,0:T(8,128)(2,1)S(1)}, u32[]{:S(2)}, u32[]{:S(2)}) collective-permute-start(bf16[2,4,128,128]{3,2,1,0:T(8,128)(2,1)S(1)} %get-tuple-element.26), channel_id=1, source_target_pairs={{2,0},{4,2},{6,4},{3,1},{5,3},{7,5},{10,8},{12,10},{14,12},{11,9},... | collective-permute-start | bytes 786440 | tf_op jit(solution)/shard_map/ppermute | solution.py:306
  31.4 0.4 shard_map.94
  31.8 1.3 %collective-permute-start.4 = (bf16[2,4,128,128]{3,2,1,0:T(8,128)(2,1)S(1)}, bf16[2,4,128,128]{3,2,1,0:T(8,128)(2,1)S(1)}, u32[]{:S(2)}, u32[]{:S(2)}) collective-permute-start(bf16[2,4,128,128]{3,2,1,0:T(8,128)(2,1)S(1)} %get-tuple-element.27), channel_id=1, source_target_pairs={{4,0},{6,2},{5,1},{7,3},{12,8},{14,10},{13,9},{15,11},{20,16},{22,... | collective-permute-start | bytes 786440 | tf_op jit(solution)/shard_map/ppermute | solution.py:306
  33.1 0.0 collective-permute-done.2.refs_4_.refs_2_
  33.1 0.6 shard_map.95
  33.6 1.3 %collective-permute-start.5 = (bf16[2,4,128,128]{3,2,1,0:T(8,128)(2,1)S(1)}, bf16[2,4,128,128]{3,2,1,0:T(8,128)(2,1)S(1)}, u32[]{:S(2)}, u32[]{:S(2)}) collective-permute-start(bf16[2,4,128,128]{3,2,1,0:T(8,128)(2,1)S(1)} %get-tuple-element.28), channel_id=1, source_target_pairs={{6,0},{7,1},{14,8},{15,9},{22,16},{23,17},{30,24},{31,25}} | collective-permute-start | bytes 786440 | tf_op jit(solution)/shard_map/ppermute | solution.py:306
  34.9 5.5 %last.1 = (bf16[128,64,128]{2,1,0:T(8,128)(2,1)}, f32[2,4,128,128]{3,2,1,0:T(8,128)S(1)}) custom-call(s32[1,2048]{1,0:T(1,128)S(1)} %get-tuple-element.17.refs_0_.start_ref, bf16[128,64,128]{2,1,0:T(8,128)(2,1)S(1)} %get-tuple-element.18.refs_1_.q_ref, bf16[128,64,128]{2,1,0:T(8,128)(2,1)S(1)} %get-tuple-element.19.refs_2_.g_ref, ...), custom_call_target="tpu_custom_call" | custom-call | flops 2147483648 | bytes 4194304 | tf_op jit(solution)/shard_map/last/pallas_call | solution.py:258
  40.4 0.0 collective-permute-done.3.refs_1_
  40.4 17.1 %collective-permute-done.4.refs_2_ = bf16[2,4,128,128]{3,2,1,0:T(8,128)(2,1)S(1)} collective-permute-done((bf16[2,4,128,128]{3,2,1,0:T(8,128)(2,1)S(1)}, bf16[2,4,128,128]{3,2,1,0:T(8,128)(2,1)S(1)}, u32[]{:S(2)}, u32[]{:S(2)}) %collective-permute-start.4) | collective-permute-done | bytes 262176 | tf_op jit(solution)/shard_map/ppermute | solution.py:306
  57.5 0.0 collective-permute-done.5.refs_3_
  57.5 0.9 %sum.1 = (bf16[128,4,128]{2,1,0:T(4,128)(2,1)}, bf16[128,4,128]{2,1,0:T(4,128)(2,1)}) custom-call(f32[2,4,128,128]{3,2,1,0:T(8,128)S(1)} %get-tuple-element.25.refs_0_, bf16[2,4,128,128]{3,2,1,0:T(8,128)(2,1)S(1)} %collective-permute-done.3.refs_1_, bf16[2,4,128,128]{3,2,1,0:T(8,128)(2,1)S(1)} %collective-permute-done.4.refs_2_, ...), custom_call_target="tpu_custom_call" | custom-call | tf_op jit(solution)/shard_map/sum/pallas_call | solution.py:287
  (1 shorter events, 0.0 us)
Async XLA Ops:
  1.7 10.5 %collective-permute-start = (bf16[2,4,128,128]{3,2,1,0:T(8,128)(2,1)S(1)}, bf16[2,4,128,128]{3,2,1,0:T(8,128)(2,1)S(1)}, u32[]{:S(2)}, u32[]{:S(2)}) collective-permute-start(bf16[2,4,128,128]{3,2,1,0:T(8,128)(2,1)S(1)} %maximum_bitcast_fusion.kv_ref), channel_id=1, source_target_pairs={{0,2},{2,4},{4,6},{1,3},{3,5},{5,7},{8,10},{10,12},{12,14},{9,11},... | collective-permute-start | bytes 786440 | tf_op jit(solution)/shard_map/ppermute | solution.py:306
  12.2 9.7 %collective-permute-start.1 = (bf16[2,4,128,128]{3,2,1,0:T(8,128)(2,1)S(1)}, bf16[2,4,128,128]{3,2,1,0:T(8,128)(2,1)S(1)}, u32[]{:S(2)}, u32[]{:S(2)}) collective-permute-start(bf16[2,4,128,128]{3,2,1,0:T(8,128)(2,1)S(1)} %collective-permute-done.kv_ref.refs_0_), channel_id=1, source_target_pairs={{0,2},{2,4},{4,6},{1,3},{3,5},{5,7},{8,10},{10,12},{12,14},{9,11},... | collective-permute-start | bytes 786440 | tf_op jit(solution)/shard_map/ppermute | solution.py:306
  18.0 9.6 %all-to-all-start = ((f32[4,2,16,128]{3,2,1,0:T(8,128)}), f32[4,2,16,128]{3,2,1,0:T(8,128)S(1)}, u32[]{:S(2)}, u32[]{:S(2)}) async-start(f32[4,2,16,128]{3,2,1,0:T(8,128)} %bitcast_bitcast_fusion), calls=%async_computation | async-start | bytes 131072 | tf_op jit(solution)/shard_map/all_to_all | solution.py:313
  21.8 11.2 %collective-permute-start.2 = (bf16[2,4,128,128]{3,2,1,0:T(8,128)(2,1)S(1)}, bf16[2,4,128,128]{3,2,1,0:T(8,128)(2,1)S(1)}, u32[]{:S(2)}, u32[]{:S(2)}) collective-permute-start(bf16[2,4,128,128]{3,2,1,0:T(8,128)(2,1)S(1)} %collective-permute-done.1.refs_4_.refs_1_), channel_id=1, source_target_pairs={{0,2},{2,4},{4,6},{1,3},{3,5},{5,7},{8,10},{10,12},{12,14},{9,11},... | collective-permute-start | bytes 786440 | tf_op jit(solution)/shard_map/ppermute | solution.py:306
  30.1 10.4 %collective-permute-start.3 = (bf16[2,4,128,128]{3,2,1,0:T(8,128)(2,1)S(1)}, bf16[2,4,128,128]{3,2,1,0:T(8,128)(2,1)S(1)}, u32[]{:S(2)}, u32[]{:S(2)}) collective-permute-start(bf16[2,4,128,128]{3,2,1,0:T(8,128)(2,1)S(1)} %get-tuple-element.26), channel_id=1, source_target_pairs={{2,0},{4,2},{6,4},{3,1},{5,3},{7,5},{10,8},{12,10},{14,12},{11,9},... | collective-permute-start | bytes 786440 | tf_op jit(solution)/shard_map/ppermute | solution.py:306
  31.8 25.8 %collective-permute-start.4 = (bf16[2,4,128,128]{3,2,1,0:T(8,128)(2,1)S(1)}, bf16[2,4,128,128]{3,2,1,0:T(8,128)(2,1)S(1)}, u32[]{:S(2)}, u32[]{:S(2)}) collective-permute-start(bf16[2,4,128,128]{3,2,1,0:T(8,128)(2,1)S(1)} %get-tuple-element.27), channel_id=1, source_target_pairs={{4,0},{6,2},{5,1},{7,3},{12,8},{14,10},{13,9},{15,11},{20,16},{22,... | collective-permute-start | bytes 786440 | tf_op jit(solution)/shard_map/ppermute | solution.py:306
  33.6 23.9 %collective-permute-start.5 = (bf16[2,4,128,128]{3,2,1,0:T(8,128)(2,1)S(1)}, bf16[2,4,128,128]{3,2,1,0:T(8,128)(2,1)S(1)}, u32[]{:S(2)}, u32[]{:S(2)}) collective-permute-start(bf16[2,4,128,128]{3,2,1,0:T(8,128)(2,1)S(1)} %get-tuple-element.28), channel_id=1, source_target_pairs={{6,0},{7,1},{14,8},{15,9},{22,16},{23,17},{30,24},{31,25}} | collective-permute-start | bytes 786440 | tf_op jit(solution)/shard_map/ppermute | solution.py:306

commit v3 on v2

--- a/solution.py
+++ b/solution.py
@@ -90,8 +90,8 @@
                 kv_ref[0, i], kv_ref[1, i], q, g, stats_ref[i, 0:1], stats_ref[i, 1:2], None
             )
             ds_ref[i] = ds
-            out_ref[0, i] = (dk * scaling).astype(jnp.bfloat16)
-            out_ref[1, i] = dv.astype(jnp.bfloat16)
+            out_ref[0, i] = (dk * scaling).astype(out_ref.dtype)
+            out_ref[1, i] = dv.astype(out_ref.dtype)
 
     @pl.when(jnp.logical_not(full))
     def _():
@@ -136,8 +136,8 @@
                 def _():
                     ds_ref[i, :, cut] = jnp.zeros((keys, step * share), jnp.bfloat16)
 
-            out_ref[0, i] = (acc_ref[0] * scaling).astype(jnp.bfloat16)
-            out_ref[1, i] = acc_ref[1].astype(jnp.bfloat16)
+            out_ref[0, i] = (acc_ref[0] * scaling).astype(out_ref.dtype)
+            out_ref[1, i] = acc_ref[1].astype(out_ref.dtype)
             return 0
 
         lax.fori_loop(0, kv_heads, one_head, 0)
@@ -183,6 +183,10 @@
     )
 
 
+def in_hbm(*arrays):
+    return [pltpu.with_memory_space_constraint(x, pltpu.HBM) for x in arrays]
+
+
 def first_past(share, docs, q, g, raw, kv):
     _, kv_heads, keys, dim = kv.shape
     rows = q.shape[0] * share
@@ -192,7 +196,7 @@
         out_specs=[VMEM] * 6,
         out_shape=[
             jax.ShapeDtypeStruct((kv_heads, keys, rows), jnp.bfloat16),
-            jax.ShapeDtypeStruct(kv.shape, jnp.bfloat16),
+            jax.ShapeDtypeStruct(kv.shape, jnp.float32),
             jax.ShapeDtypeStruct(q.shape, q.dtype),
             jax.ShapeDtypeStruct(g.shape, g.dtype),
             jax.ShapeDtypeStruct((kv_heads, 2, rows), jnp.float32),
@@ -205,10 +209,10 @@
             pltpu.SemaphoreType.DMA((kv_heads,)),
             pltpu.SemaphoreType.DMA((kv_heads,)),
         ],
-        compiler_params=pltpu.CompilerParams(vmem_limit_bytes=47 * MIB),
+        compiler_params=pltpu.CompilerParams(vmem_limit_bytes=32 * MIB),
         cost_estimate=past_cost(kv, rows),
         name="past_1",
-    )(docs, q, g, raw, kv)
+    )(*in_hbm(docs, q, g), raw, kv)
 
 
 def next_past(shift, share, start, q, g, stats, kv):
@@ -301,26 +305,28 @@
     per_dev = heads // groups
     reach = min(groups - 1, -(-(DOC_MAX - 1) // tok))
 
-    def moved(x, s):
-        pairs = [(i, i + s) for i in range(groups) if 0 <= i + s < groups]
+    def moved(x, s, first=0):
+        pairs = [(i, i + s) for i in range(first, groups) if 0 <= i + s < groups]
         return lax.ppermute(x, "ctx", pairs)
 
     kvs = [jnp.stack([key_rows, value_rows]).transpose(0, 2, 1, 3)]
-    for _ in range(1, reach + 1):
-        kvs.append(moved(kvs[-1], 1))
+    for s in range(1, reach + 1):
+        kvs.append(moved(kvs[1], 1, 1) if s == 2 else moved(kvs[0], s))
     raw = jnp.stack([log_norm[0], softmax_delta[0]])
     raw = raw.reshape(2, per_dev, groups, tok).transpose(2, 0, 1, 3)
     raw = lax.all_to_all(raw, "ctx", split_axis=0, concat_axis=0, tiled=True)
     raw = raw.reshape(kv_heads, groups // kv_heads, 2, per_dev, tok)
     raw = raw.transpose(0, 2, 1, 3, 4).reshape(kv_heads, 2, share, tok)
-    docs = jnp.maximum(doc_lengths, 1)
-    ds, part, q, g, stats, start = first_past(share, docs, query_rows, out_grad, raw, kvs[1])
-    terms = [moved(part, -1)]
-    ds_list = [ds]
+    ds, near, q, g, stats, start = first_past(share, doc_lengths, query_rows, out_grad, raw, kvs[1])
+    ds_list, terms = [ds], []
     for s in range(2, reach + 1):
         ds, part = next_past(s, share, start, q, g, stats, kvs[s])
         ds_list.append(ds)
-        terms.append(moved(part, -s))
+        if s == 2:
+            near = near + moved(part, -1, 2).astype(jnp.float32)
+        else:
+            terms.append(moved(part, -s))
+    terms.append(moved(near.astype(jnp.bfloat16), -1))
     query_grad, total = last_grads(share, start, q, g, stats, kvs, ds_list)
     key_grad, value_grad = sum_terms(total, terms)
     return (query_grad, key_grad, value_grad)

time: 58.8 us -> 54.9 us (0.934)
  waiting for transfers between devices: 23.5 us -> 19.3 us
  starting transfers between devices: 21.3 us -> 22.2 us
  other arithmetic: 2.1 us -> 1.5 us
    all_to_all x1, starting transfers between devices: 3.85 us -> 7.57 us  [local(): raw = lax.all_to_all(raw, 'ctx', split_axis=0, concat_axis=0, tiled=True)]
    ppermute x6, waiting for transfers between devices: 22.6 us -> 19.3 us  [moved(): return lax.ppermute(x, 'ctx', pairs)]
    ppermute x6, starting transfers between devices: 17.4 us -> 14.6 us  [moved(): return lax.ppermute(x, 'ctx', pairs)]
    all_to_all x1, waiting for transfers between devices: 0.87 us -> 0.01 us  [local(): raw = lax.all_to_all(raw, 'ctx', split_axis=0, concat_axis=0, tiled=True)]
    max x1 -> x0, other arithmetic: 0.66 us -> none  [local(): docs = jnp.maximum(doc_lengths, 1)]
  transfers between devices with their start and end apart: 7 -> 7, of which waited for: 3 -> 4; matrix products, arithmetic and copies ran while one was open for 4% -> 3% of each run, Pallas kernels for 15% -> 16%
where the time goes in v3:
time: 54.9 us; the launch traced here: 54.5 us
  starting transfers between devices  22.2 us (40%)
  waiting for transfers between devices  19.3 us (35%)
  Pallas kernels  9.77 us (18%)
  other arithmetic  1.5 us (3%)
  local copies, waits for them, and re-layouts  1 us (2%)
  between operations  0.74 us (1%)
    ppermute x6, waiting for transfers between devices, moved(): return lax.ppermute(x, 'ctx', pairs)  19.3 us
    ppermute x6, starting transfers between devices, moved(): return lax.ppermute(x, 'ctx', pairs)  14.6 us
    all_to_all x1, starting transfers between devices, local(): raw = lax.all_to_all(raw, 'ctx', split_axis=0, concat_axis=0, tiled=True)  7.57 us
    pallas_call x1, Pallas kernels, last_grads(): pl.pallas_call(functools.partial(last_kernel, share), in_specs=[VMEM] * (...  5.49 us
    pallas_call x1, Pallas kernels, first_past(): pl.pallas_call(functools.partial(first_past_kernel, share), in_specs=[HBM...  2.46 us
    transpose x1, other arithmetic, local(): raw = raw.reshape(2, per_dev, groups, tok).transpose(2, 0, 1, 3)  1.41 us
  transfers between devices with their start and end apart: 7, of which 4 were waited for; matrix products, arithmetic and copies ran while one was open for 3% of the time, Pallas kernels for 16%

profile of v3, /device:TPU:0, one launch (start us, length us, event | category | flops | bytes accessed | tf_op | source)
XLA Modules:
  0.0 54.5 jit_solution(8535184882413256971)
XLA Ops:
  0.6 1.0 %copy_bitcast_fusion = (bf16[1,128,4,128]{3,1,2,0:T(8,128)(2,1)S(1)}, bf16[1,128,4,128]{3,1,2,0:T(8,128)(2,1)S(1)}) fusion(bf16[128,4,128]{2,1,0:T(4,128)(2,1)} %param.9, bf16[128,4,128]{2,1,0:T(4,128)(2,1)} %param.8), kind=kLoop, calls=%fused_computation.2 | loop fusion | bytes 524288 | tf_op jit(solution)/shard_map/stack | solution.py:312
  1.7 5.0 %collective-permute-start = (bf16[2,4,128,128]{3,2,1,0:T(8,128)(2,1)S(1)}, bf16[2,4,128,128]{3,2,1,0:T(8,128)(2,1)S(1)}, u32[]{:S(2)}, u32[]{:S(2)}) collective-permute-start(bf16[2,4,128,128]{3,2,1,0:T(8,128)(2,1)S(1)} %maximum_bitcast_fusion.kv_ref), channel_id=1, source_target_pairs={{0,2},{2,4},{4,6},{1,3},{3,5},{5,7},{8,10},{10,12},{12,14},{9,11},... | collective-permute-start | bytes 786440 | tf_op jit(solution)/shard_map/ppermute | solution.py:310
  6.7 5.5 %collective-permute-done.kv_ref.refs_0_ = bf16[2,4,128,128]{3,2,1,0:T(8,128)(2,1)S(1)} collective-permute-done((bf16[2,4,128,128]{3,2,1,0:T(8,128)(2,1)S(1)}, bf16[2,4,128,128]{3,2,1,0:T(8,128)(2,1)S(1)}, u32[]{:S(2)}, u32[]{:S(2)}) %collective-permute-start) | collective-permute-done | bytes 262176 | tf_op jit(solution)/shard_map/ppermute | solution.py:310
  12.2 0.7 %collective-permute-start.1 = (bf16[2,4,128,128]{3,2,1,0:T(8,128)(2,1)S(1)}, bf16[2,4,128,128]{3,2,1,0:T(8,128)(2,1)S(1)}, u32[]{:S(2)}, u32[]{:S(2)}) collective-permute-start(bf16[2,4,128,128]{3,2,1,0:T(8,128)(2,1)S(1)} %collective-permute-done.kv_ref.refs_0_), channel_id=1, source_target_pairs={{2,4},{4,6},{3,5},{5,7},{10,12},{12,14},{11,13},{13,15},{18,20},{2... | collective-permute-start | bytes 786440 | tf_op jit(solution)/shard_map/ppermute | solution.py:310
  12.9 1.4 %bitcast_bitcast_fusion = f32[4,2,16,128]{3,2,1,0:T(8,128)} fusion(f32[1,16,512]{2,1,0:T(8,128)} %param.11, f32[1,16,512]{2,1,0:T(8,128)} %param.12), kind=kLoop, calls=%fused_computation.4 | loop fusion | flops 16384 | bytes 131072 | tf_op jit(solution)/shard_map/transpose | solution.py:316
  14.3 7.6 %all-to-all-start = ((f32[4,2,16,128]{3,2,1,0:T(8,128)}), f32[4,2,16,128]{3,2,1,0:T(8,128)S(1)}, u32[]{:S(2)}, u32[]{:S(2)}) async-start(f32[4,2,16,128]{3,2,1,0:T(8,128)} %bitcast_bitcast_fusion), calls=%async_computation | async-start | bytes 131072 | tf_op jit(solution)/shard_map/all_to_all | solution.py:317
  21.8 5.7 %collective-permute-start.2 = (bf16[2,4,128,128]{3,2,1,0:T(8,128)(2,1)S(1)}, bf16[2,4,128,128]{3,2,1,0:T(8,128)(2,1)S(1)}, u32[]{:S(2)}, u32[]{:S(2)}) collective-permute-start(bf16[2,4,128,128]{3,2,1,0:T(8,128)(2,1)S(1)} %maximum_bitcast_fusion.kv_ref), channel_id=1, source_target_pairs={{0,6},{1,7},{8,14},{9,15},{16,22},{17,23},{24,30},{25,31}} | collective-permute-start | bytes 786440 | tf_op jit(solution)/shard_map/ppermute | solution.py:310
  27.6 0.0 all-to-all-done.raw_ref
  27.6 2.5 %past_1.1 = (bf16[4,128,2048]{2,1,0:T(8,128)(2,1)S(1)}, f32[2,4,128,128]{3,2,1,0:T(8,128)S(1)}, bf16[128,64,128]{2,1,0:T(8,128)(2,1)S(1)}, bf16[128,64,128]{2,1,...) custom-call(s32[3]{0:T(128)} %docs_hbm.1, bf16[128,64,128]{2,1,0:T(8,128)(2,1)} %q_hbm.1, ...), custom_call_target="tpu_custom_call" | custom-call | flops 1073741824 | bytes 4194304 | tf_op jit(solution)/shard_map/past_1/pallas_call | solution.py:193
  30.1 0.0 collective-permute-done.1.refs_4_.refs_1_
  30.1 0.4 shard_map.94
  30.5 0.7 %collective-permute-start.4 = (bf16[2,4,128,128]{3,2,1,0:T(8,128)(2,1)S(1)}, bf16[2,4,128,128]{3,2,1,0:T(8,128)(2,1)S(1)}, u32[]{:S(2)}, u32[]{:S(2)}) collective-permute-start(bf16[2,4,128,128]{3,2,1,0:T(8,128)(2,1)S(1)} %get-tuple-element.28), channel_id=1, source_target_pairs={{4,2},{6,4},{5,3},{7,5},{12,10},{14,12},{13,11},{15,13},{20,18},{2... | collective-permute-start | bytes 786440 | tf_op jit(solution)/shard_map/ppermute | solution.py:310
  31.2 0.3 collective-permute-done.2.refs_4_.refs_2_
  31.4 0.6 %shard_map.95 = (bf16[4,128,2048]{2,1,0:T(8,128)(2,1)S(1)}, bf16[2,4,128,128]{3,2,1,0:T(8,128)(2,1)S(1)}) custom-call(s32[1,2048]{1,0:T(1,128)S(1)} %get-tuple-element.17.refs_0_.start_ref, bf16[128,64,128]{2,1,0:T(8,128)(2,1)S(1)} %get-tuple-element.18.refs_1_.q_ref, bf16[128,64,128]{2,1,0:T(8,128)(2,1)S(1)} %get-tuple-element.19.refs_2_.g_ref, ...), custom_call_target="tpu_custom_call" | custom-call | flops 1073741824 | bytes 4194304 | tf_op jit(solution)/shard_map/pallas_call | solution.py:221
  32.0 1.3 %collective-permute-start.3 = (bf16[2,4,128,128]{3,2,1,0:T(8,128)(2,1)S(1)}, bf16[2,4,128,128]{3,2,1,0:T(8,128)(2,1)S(1)}, u32[]{:S(2)}, u32[]{:S(2)}) collective-permute-start(bf16[2,4,128,128]{3,2,1,0:T(8,128)(2,1)S(1)} %get-tuple-element.26), channel_id=1, source_target_pairs={{6,0},{7,1},{14,8},{15,9},{22,16},{23,17},{30,24},{31,25}} | collective-permute-start | bytes 786440 | tf_op jit(solution)/shard_map/ppermute | solution.py:310
  33.3 0.0 collective-permute-done.4
  33.3 0.1 add_convert_fusion
  33.4 1.3 %collective-permute-start.5 = (bf16[2,4,128,128]{3,2,1,0:T(8,128)(2,1)S(1)}, bf16[2,4,128,128]{3,2,1,0:T(8,128)(2,1)S(1)}, u32[]{:S(2)}, u32[]{:S(2)}) collective-permute-start(bf16[2,4,128,128]{3,2,1,0:T(8,128)(2,1)S(1)} %add_convert_fusion), channel_id=1, source_target_pairs={{2,0},{4,2},{6,4},{3,1},{5,3},{7,5},{10,8},{12,10},{14,12},{11,9},... | collective-permute-start | bytes 786440 | tf_op jit(solution)/shard_map/ppermute | solution.py:310
  34.7 5.5 %last.1 = (bf16[128,64,128]{2,1,0:T(8,128)(2,1)}, f32[2,4,128,128]{3,2,1,0:T(8,128)S(1)}) custom-call(s32[1,2048]{1,0:T(1,128)S(1)} %get-tuple-element.17.refs_0_.start_ref, bf16[128,64,128]{2,1,0:T(8,128)(2,1)S(1)} %get-tuple-element.18.refs_1_.q_ref, bf16[128,64,128]{2,1,0:T(8,128)(2,1)S(1)} %get-tuple-element.19.refs_2_.g_ref, ...), custom_call_target="tpu_custom_call" | custom-call | flops 2147483648 | bytes 4194304 | tf_op jit(solution)/shard_map/last/pallas_call | solution.py:262
  40.2 10.9 %collective-permute-done.3.refs_1_ = bf16[2,4,128,128]{3,2,1,0:T(8,128)(2,1)S(1)} collective-permute-done((bf16[2,4,128,128]{3,2,1,0:T(8,128)(2,1)S(1)}, bf16[2,4,128,128]{3,2,1,0:T(8,128)(2,1)S(1)}, u32[]{:S(2)}, u32[]{:S(2)}) %collective-permute-start.3) | collective-permute-done | bytes 262176 | tf_op jit(solution)/shard_map/ppermute | solution.py:310
  51.0 2.6 %collective-permute-done.5.refs_2_ = bf16[2,4,128,128]{3,2,1,0:T(8,128)(2,1)S(1)} collective-permute-done((bf16[2,4,128,128]{3,2,1,0:T(8,128)(2,1)S(1)}, bf16[2,4,128,128]{3,2,1,0:T(8,128)(2,1)S(1)}, u32[]{:S(2)}, u32[]{:S(2)}) %collective-permute-start.5) | collective-permute-done | bytes 262176 | tf_op jit(solution)/shard_map/ppermute | solution.py:310
  53.7 0.9 %sum.1 = (bf16[128,4,128]{2,1,0:T(4,128)(2,1)}, bf16[128,4,128]{2,1,0:T(4,128)(2,1)}) custom-call(f32[2,4,128,128]{3,2,1,0:T(8,128)S(1)} %get-tuple-element.25.refs_0_, bf16[2,4,128,128]{3,2,1,0:T(8,128)(2,1)S(1)} %collective-permute-done.3.refs_1_, bf16[2,4,128,128]{3,2,1,0:T(8,128)(2,1)S(1)} %collective-permute-done.5.refs_2_), custom_call_target="tpu_custom_call" | custom-call | tf_op jit(solution)/shard_map/sum/pallas_call | solution.py:291
  (1 shorter events, 0.0 us)
Async XLA Ops:
  1.7 10.5 %collective-permute-start = (bf16[2,4,128,128]{3,2,1,0:T(8,128)(2,1)S(1)}, bf16[2,4,128,128]{3,2,1,0:T(8,128)(2,1)S(1)}, u32[]{:S(2)}, u32[]{:S(2)}) collective-permute-start(bf16[2,4,128,128]{3,2,1,0:T(8,128)(2,1)S(1)} %maximum_bitcast_fusion.kv_ref), channel_id=1, source_target_pairs={{0,2},{2,4},{4,6},{1,3},{3,5},{5,7},{8,10},{10,12},{12,14},{9,11},... | collective-permute-start | bytes 786440 | tf_op jit(solution)/shard_map/ppermute | solution.py:310
  12.2 17.9 %collective-permute-start.1 = (bf16[2,4,128,128]{3,2,1,0:T(8,128)(2,1)S(1)}, bf16[2,4,128,128]{3,2,1,0:T(8,128)(2,1)S(1)}, u32[]{:S(2)}, u32[]{:S(2)}) collective-permute-start(bf16[2,4,128,128]{3,2,1,0:T(8,128)(2,1)S(1)} %collective-permute-done.kv_ref.refs_0_), channel_id=1, source_target_pairs={{2,4},{4,6},{3,5},{5,7},{10,12},{12,14},{11,13},{13,15},{18,20},{2... | collective-permute-start | bytes 786440 | tf_op jit(solution)/shard_map/ppermute | solution.py:310
  14.3 13.3 %all-to-all-start = ((f32[4,2,16,128]{3,2,1,0:T(8,128)}), f32[4,2,16,128]{3,2,1,0:T(8,128)S(1)}, u32[]{:S(2)}, u32[]{:S(2)}) async-start(f32[4,2,16,128]{3,2,1,0:T(8,128)} %bitcast_bitcast_fusion), calls=%async_computation | async-start | bytes 131072 | tf_op jit(solution)/shard_map/all_to_all | solution.py:317
  21.8 9.6 %collective-permute-start.2 = (bf16[2,4,128,128]{3,2,1,0:T(8,128)(2,1)S(1)}, bf16[2,4,128,128]{3,2,1,0:T(8,128)(2,1)S(1)}, u32[]{:S(2)}, u32[]{:S(2)}) collective-permute-start(bf16[2,4,128,128]{3,2,1,0:T(8,128)(2,1)S(1)} %maximum_bitcast_fusion.kv_ref), channel_id=1, source_target_pairs={{0,6},{1,7},{8,14},{9,15},{16,22},{17,23},{24,30},{25,31}} | collective-permute-start | bytes 786440 | tf_op jit(solution)/shard_map/ppermute | solution.py:310
  30.5 2.8 %collective-permute-start.4 = (bf16[2,4,128,128]{3,2,1,0:T(8,128)(2,1)S(1)}, bf16[2,4,128,128]{3,2,1,0:T(8,128)(2,1)S(1)}, u32[]{:S(2)}, u32[]{:S(2)}) collective-permute-start(bf16[2,4,128,128]{3,2,1,0:T(8,128)(2,1)S(1)} %get-tuple-element.28), channel_id=1, source_target_pairs={{4,2},{6,4},{5,3},{7,5},{12,10},{14,12},{13,11},{15,13},{20,18},{2... | collective-permute-start | bytes 786440 | tf_op jit(solution)/shard_map/ppermute | solution.py:310
  32.0 19.0 %collective-permute-start.3 = (bf16[2,4,128,128]{3,2,1,0:T(8,128)(2,1)S(1)}, bf16[2,4,128,128]{3,2,1,0:T(8,128)(2,1)S(1)}, u32[]{:S(2)}, u32[]{:S(2)}) collective-permute-start(bf16[2,4,128,128]{3,2,1,0:T(8,128)(2,1)S(1)} %get-tuple-element.26), channel_id=1, source_target_pairs={{6,0},{7,1},{14,8},{15,9},{22,16},{23,17},{30,24},{31,25}} | collective-permute-start | bytes 786440 | tf_op jit(solution)/shard_map/ppermute | solution.py:310
  33.4 20.3 %collective-permute-start.5 = (bf16[2,4,128,128]{3,2,1,0:T(8,128)(2,1)S(1)}, bf16[2,4,128,128]{3,2,1,0:T(8,128)(2,1)S(1)}, u32[]{:S(2)}, u32[]{:S(2)}) collective-permute-start(bf16[2,4,128,128]{3,2,1,0:T(8,128)(2,1)S(1)} %add_convert_fusion), channel_id=1, source_target_pairs={{2,0},{4,2},{6,4},{3,1},{5,3},{7,5},{10,8},{12,10},{14,12},{11,9},... | collective-permute-start | bytes 786440 | tf_op jit(solution)/shard_map/ppermute | solution.py:310
